TPU v7x, 128 devices: a whole 4x4x4 slice. The times are simulated.
128 devices in a mesh: row: 8 (over y_hi, x), col: 16 (over z, y_lo, core).
Axes of the slice: x: 4, y: 4 (y_hi: 2, y_lo: 2; y = y_hi * 2 + y_lo), z: 4, core: 2. Of those that a mesh axis runs over, the one named last changes fastest.
Arguments:
- amps: float32 [4096, 9216], P('row', 'col'), may hold values from -6 to 6
- ladder_ints: float32 [4096, 4096], P('row', 'col'), may hold values from -0.25 to 0.25
- cycle_ints: float32 [6144, 6144], P(None, 'row'), may hold values from -0.21875 to 0.21875
- virt_irrep: int32 [64], replicated, may hold values from 0 to 7
- occ_irrep: int32 [96], replicated, may hold values from 0 to 7
- virt_energy: float32 [64], replicated, may hold values from 0.5 to 3
- occ_energy: float32 [96], replicated, may hold values from -3 to -0.5
Outputs:
- update: float32 [4096, 9216], P('row', 'col')
All inputs are finite; a program needn't handle non-finite values.
Results may differ from a plain program's by a relative error of at most 0.00005.
Values sent between devices are 32-bit elements; how exact they have to be, the bound alone decides.
A program may use at most 128 MiB of HBM per device.

v0:
```python
import jax
import jax.numpy as jnp
from jax import lax
from jax.sharding import PartitionSpec as P


def pair_labels(first, second):
    return jnp.bitwise_xor(first[:, None], second[None, :]).reshape(-1)


def body(amps, ladder_ints, cycle_ints, virt_irrep, occ_irrep, virt_energy, occ_energy):
    highest = lax.Precision.HIGHEST
    row_count = lax.axis_size("row")
    col_count = lax.axis_size("col")
    row_index = lax.axis_index("row")
    col_index = lax.axis_index("col")
    virt_total = virt_irrep.shape[0]
    occ_total = occ_irrep.shape[0]
    virt_local = virt_total // row_count
    occ_local = occ_total // col_count
    virt_cols = virt_total // col_count
    pair_rows = amps.shape[0]
    virt_pairs = pair_labels(virt_irrep, virt_irrep)
    own_pairs = lax.dynamic_slice_in_dim(virt_pairs, row_index * pair_rows, pair_rows)
    rows_full = lax.all_gather(ladder_ints, "col", axis=1, tiled=True)
    masked = jnp.where(own_pairs[:, None] == virt_pairs[None, :], rows_full, jnp.float32(0.0))
    ladder = jnp.dot(
        masked,
        lax.all_gather(amps, "row", axis=0, tiled=True),
        precision=highest,
        preferred_element_type=jnp.float32,
    )
    blocks = amps.reshape(virt_local, virt_total, occ_local, occ_total)
    moved = lax.all_to_all(blocks, "col", split_axis=1, concat_axis=2, tiled=True)
    cycle_amps = moved.transpose(0, 2, 1, 3).reshape(virt_local * occ_total, virt_cols * occ_total)
    mixed_pairs = pair_labels(virt_irrep, occ_irrep)
    cycle_rows = cycle_amps.shape[0]
    own_mixed = lax.dynamic_slice_in_dim(mixed_pairs, row_index * cycle_rows, cycle_rows)
    part = cycle_ints
    part = jnp.where(mixed_pairs[:, None] == own_mixed[None, :], part, jnp.float32(0.0))
    cycle = lax.psum_scatter(
        jnp.dot(part, cycle_amps, precision=highest, preferred_element_type=jnp.float32),
        "row",
        scatter_dimension=0,
        tiled=True,
    )
    cycle_blocks = cycle.reshape(virt_local, occ_total, virt_cols, occ_total)
    returned = lax.all_to_all(cycle_blocks, "col", split_axis=1, concat_axis=2, tiled=True)
    cycle_back = returned.transpose(0, 2, 1, 3).reshape(
        virt_local * virt_total, occ_local * occ_total
    )
    own_virt = lax.dynamic_slice_in_dim(virt_energy, row_index * virt_local, virt_local)
    own_occ = lax.dynamic_slice_in_dim(occ_energy, col_index * occ_local, occ_local)
    row_energy = (own_virt[:, None] + virt_energy[None, :]).reshape(-1)
    col_energy = (own_occ[:, None] + occ_energy[None, :]).reshape(-1)
    return (ladder + cycle_back) / (row_energy[:, None] - col_energy[None, :])


def solution(mesh):
    placed = (P("row", "col"), P("row", "col"), P(None, "row"), P(), P(), P(), P())
    return jax.shard_map(
        body, mesh=mesh, in_specs=placed, out_specs=P("row", "col"), check_vma=False
    )
```

profile of v0, /device:TPU:0, one launch (start us, length us, event | category | flops | bytes accessed | tf_op | source)
XLA Modules:
  0.0 342.1 jit_solution(9662169634818703295)
XLA Ops:
  7.4 1.6 reshape.87
  9.0 1.8 copy.24
  10.8 6.7 %all-to-all-start = ((f32[8,64,6,96]{3,0,2,1:T(8,128)}), f32[8,64,6,96]{3,0,2,1:T(8,128)S(1)}, u32[]{:S(2)}, u32[]{:S(2)}) async-start(f32[8,64,6,96]{3,0,2,1:T(8,128)} %copy.24), calls=%async_computation | async-start | bytes 3145728 | tf_op jit(solution)/shard_map/all_to_all | solution.py:34
  17.6 0.1 broadcast_xor_fusion
  17.6 0.1 xor.49
  17.7 0.1 dynamic_slice.13
  17.8 21.9 %all-to-all-done = f32[8,64,6,96]{3,0,2,1:T(8,128)S(1)} async-done(((f32[8,64,6,96]{3,0,2,1:T(8,128)}), f32[8,64,6,96]{3,0,2,1:T(8,128)S(1)}, u32[]{:S(2)}, u32[]{:S(2)}) %all-to-all-start) | async-done | bytes 1179680 | tf_op jit(solution)/shard_map/all_to_all | solution.py:34
  39.7 0.1 copy.25
  39.8 0.7 copy.26
  40.5 0.5 reshape.84
  41.0 35.1 %fusion = f32[6144,384]{1,0:T(8,128)} fusion(f32[768,384]{0,1:T(8,128)S(1)} %reshape.84, f32[6144,768]{1,0:T(8,128)} %param.9, s32[768]{0:T(1024)S(1)} %dynamic_slice.13, s32[6144]{0:T(1024)S(1)} %xor.49), kind=kOutput, calls=%fused_computation | convolution fusion | flops 21752709120 | bytes 29518848 | tf_op jit(solution)/shard_map/dot_general | solution.py:42
  76.2 0.5 all-gather.3.cloned.1.call-update
  76.8 0.5 all-gather.5.cloned.1.call-update
  77.4 149.9 %reduce-scatter.2.cloned.1.call-done = f32[768,384]{1,0:T(8,128)} async-done(((f32[6144,384]{1,0:T(8,128)}), f32[768,384]{1,0:T(8,128)}) %reduce-scatter.2.cloned.1.call-update) | async-done | bytes 1179664 | tf_op jit(solution)/shard_map/reduce_scatter | solution.py:41
  227.3 2.2 reshape.85
  229.5 2.1 copy.27
  231.6 5.8 %all-to-all-start.1 = ((f32[8,96,4,96]{3,0,2,1:T(8,128)}), f32[8,96,4,96]{3,0,2,1:T(8,128)S(1)}, u32[]{:S(2)}, u32[]{:S(2)}) async-start(f32[8,96,4,96]{3,0,2,1:T(8,128)} %copy.27), calls=%async_computation.2 | async-start | bytes 3145728 | tf_op jit(solution)/shard_map/all_to_all | solution.py:48
  237.4 0.1 broadcast_xor_fusion.1
  237.4 0.1 xor.45
  237.5 0.1 dynamic_slice.14
  237.6 0.1 broadcast_add_fusion.1
  237.7 0.7 add.64
  238.3 0.1 dynamic_slice.15
  238.4 0.1 broadcast_add_fusion
  238.5 0.7 add.69
  239.2 0.7 dynamic_slice.12
  239.8 36.9 %all-to-all-done.1 = f32[8,96,4,96]{3,0,2,1:T(8,128)S(1)} async-done(((f32[8,96,4,96]{3,0,2,1:T(8,128)}), f32[8,96,4,96]{3,0,2,1:T(8,128)S(1)}, u32[]{:S(2)}, u32[]{:S(2)}) %all-to-all-start.1) | async-done | bytes 1179680 | tf_op jit(solution)/shard_map/all_to_all | solution.py:48
  276.7 1.3 copy.28
  278.0 2.0 copy.33
  280.0 0.5 reshape.88
  280.6 34.2 %all-gather.5.cloned.1.call-done = f32[4096,576]{0,1:T(8,128)} async-done(((f32[512,576]{0,1:T(8,128)}), f32[4096,576]{0,1:T(8,128)}) %all-gather.5.cloned.1.call-update) | async-done | bytes 9437200 | tf_op jit(solution)/shard_map/all_gather | solution.py:29
  314.8 19.8 %fusion.15 = f32[512,576]{0,1:T(8,128)} fusion(f32[512,576]{0,1:T(8,128)S(1)} %reshape.88, f32[4096,576]{0,1:T(8,128)} %all-gather.5.cloned.1.call-done, f32[512,4096]{1,0:T(8,128)} %all-gather.3.cloned.1.call-done, s32[4096]{0:T(1024)S(1)} %xor.45, s32[512]{0:T(512)} %dynamic_slice.12, f32[576]{0:T(1024)} %add.69, f32[512]{0:T(512)} %add.64), kind=kOutput, calls=%fused_computation.13 | convolution fusion | flops 14500593664 | bytes 20207872 | tf_op jit(solution)/shard_map/dot_general | solution.py:27
  (13 shorter events, 0.2 us)
Async XLA Ops:
  10.8 6.7 %copy-start = (s32[64]{0:T(128)S(1)}, s32[64]{0:T(128)}, u32[]{:S(2)}) copy-start(s32[64]{0:T(128)} %param.10) | copy-start | bytes 772
  10.8 6.8 %copy-start.1 = (s32[96]{0:T(128)S(1)}, s32[96]{0:T(128)}, u32[]{:S(2)}) copy-start(s32[96]{0:T(128)} %param.11) | copy-start | bytes 1156
  10.8 28.9 %all-to-all-start = ((f32[8,64,6,96]{3,0,2,1:T(8,128)}), f32[8,64,6,96]{3,0,2,1:T(8,128)S(1)}, u32[]{:S(2)}, u32[]{:S(2)}) async-start(f32[8,64,6,96]{3,0,2,1:T(8,128)} %copy.24), calls=%async_computation | async-start | bytes 3145728 | tf_op jit(solution)/shard_map/all_to_all | solution.py:34
  17.5 209.8 %reduce-scatter.2.cloned.1.call-start = ((), (), s32[]{:S(2)}) async-start(), calls=%async_computation.5 | async-start | bytes 10616832 | tf_op jit(solution)/shard_map/reduce_scatter | solution.py:41
  76.2 204.4 %all-gather.3.cloned.1.call-start = ((), (), s32[]{:S(2)}) async-start(), calls=%async_computation.3 | async-start | bytes 8912896 | tf_op jit(solution)/shard_map/all_gather | solution.py:25
  76.8 238.1 %all-gather.5.cloned.1.call-start = ((), (), s32[]{:S(2)}) async-start(), calls=%async_computation.4 | async-start | bytes 10616832 | tf_op jit(solution)/shard_map/all_gather | solution.py:29
  231.6 5.9 %copy-start.2 = (f32[64]{0:T(128)S(1)}, f32[64]{0:T(128)}, u32[]{:S(2)}) copy-start(f32[64]{0:T(128)} %param.12) | copy-start | bytes 772
  231.6 6.8 %copy-start.3 = (f32[96]{0:T(128)S(1)}, f32[96]{0:T(128)}, u32[]{:S(2)}) copy-start(f32[96]{0:T(128)} %param.13) | copy-start | bytes 1156
  231.6 45.1 %all-to-all-start.1 = ((f32[8,96,4,96]{3,0,2,1:T(8,128)}), f32[8,96,4,96]{3,0,2,1:T(8,128)S(1)}, u32[]{:S(2)}, u32[]{:S(2)}) async-start(f32[8,96,4,96]{3,0,2,1:T(8,128)} %copy.27), calls=%async_computation.2 | async-start | bytes 3145728 | tf_op jit(solution)/shard_map/all_to_all | solution.py:48
Sparse Core Ops, SparseCore 0:
  76.3 150.9 reduce-scatter.1
Sparse Core Ops, SparseCore 1:
  78.3 87.5 all-gather.2
  168.1 146.6 all-gather.4
where the time goes:
time: 342 us
  waiting for transfers between devices  244 us (71%)
  matrix products  54.9 us (16%)
  local copies, waits for them, and re-layouts  15.3 us (4%)
  between operations  15 us (4%)
  starting transfers between devices  12.6 us (4%)
    reduce_scatter x1, waiting for transfers between devices, body(): lax.psum_scatter(jnp.dot(part, cycle_amps, precision=highest, preferred_e...  150 us
    all_to_all x1, waiting for transfers between devices, body(): lax.all_to_all(cycle_blocks, 'col', split_axis=1, concat_axis=2, tiled=True)  36.9 us
    dot_general x1, matrix products, body(): jnp.dot(part, cycle_amps, precision=highest, preferred_element_type=jnp.f...  35.1 us
    all_gather x1, waiting for transfers between devices, body(): lax.all_gather(amps, 'row', axis=0, tiled=True)  34.2 us
    all_to_all x1, waiting for transfers between devices, body(): lax.all_to_all(blocks, 'col', split_axis=1, concat_axis=2, tiled=True)  21.9 us
    dot_general x1, matrix products, body(): jnp.dot(masked, lax.all_gather(amps, 'row', axis=0, tiled=True), precisio...  19.8 us
  transfers between devices with their start and end apart: 5, of which 4 were waited for; matrix products, arithmetic and copies ran while one was open for 3% of the time, Pallas kernels for 0%

commit v1 on v0

v1 whole, which is shorter than its diff:
```python
import functools

import jax
import jax.numpy as jnp
import numpy as np
from jax import lax
from jax.experimental import pallas as pl
from jax.experimental.pallas import tpu as pltpu
from jax.sharding import PartitionSpec as P

MESH = pl.DeviceIdType.MESH
F32, BF16 = jnp.float32, jnp.bfloat16

VT, OT = 64, 96
VL, OL, VC = 8, 6, 4
CK = VL * OT
BJ = VC * OT
BLK = VL * OL
AB = VL * VT
CD = 256
HIJ = OL * OT // 2

A2A, BACK = 0, 16
YT, X1, X2, LY, LZ, LZ2, LC, OB = 32, 33, 35, 37, 40, 42, 44, 48
RS, YR = 49, 55
NSEM = 56


def split2(value):
    high = value.astype(BF16)
    low = (value - high.astype(F32)).astype(BF16)
    return high, low


def dot(a, b):
    return jnp.dot(a, b, preferred_element_type=F32)


def dot_nt(a, b):
    return lax.dot_general(a, b, (((1,), (1,)), ((), ())), preferred_element_type=F32)


def kernel(
    virt_ref, s_ref, tt_ref, l_ref, w_ref, ml_ref, vl_ref, oi_ref, vb_ref, p_ref, q_ref,
    lo_ref, d_ref,
    tx, lx, ca, ca_hi, ca_lo, wbuf, w_hi, w_lo, part, recv, yrecv, oacc, l_hi, l_lo, cp,
    ssem, rsem, wsem, lsem,
):
    row, col = lax.axis_index("row"), lax.axis_index("col")
    yh, x = row // 4, row % 4
    z, yl, core = col // 4, (col // 2) % 2, col % 2
    yme = yh * 2 + yl
    xp, xm, xo = (x + 1) % 4, (x + 3) % 4, (x + 2) % 4
    zp, zm, zo = (z + 1) % 4, (z + 3) % 4, (z + 2) % 4
    right, left = (yh * 4 + xp, col), (yh * 4 + xm, col)
    up, down = (row, zp * 4 + col % 4), (row, zm * 4 + col % 4)
    yrow = (1 - yh) * 4 + x
    ycol = z * 4 + (1 - yl) * 2 + core
    opp = (yrow, col)
    mate = (row, z * 4 + yl * 2 + (1 - core))

    def rc(src, dst, k, dev):
        return pltpu.make_async_remote_copy(
            src_ref=src, dst_ref=dst, send_sem=ssem.at[k], recv_sem=rsem.at[k],
            device_id=dev, device_id_type=MESH,
        )

    def rows48(ref, index):
        return ref.at[pl.ds(pl.multiple_of(index * BLK, BLK), BLK), :]

    bar = pltpu.get_barrier_semaphore()

    def greet(d, carry):
        pl.semaphore_signal(bar, inc=1, device_id=(row, col ^ d), device_id_type=MESH)
        return carry

    lax.fori_loop(1, 16, greet, 0)
    for dev in (right, left, up, down, opp, (yrow, ycol)):
        pl.semaphore_signal(bar, inc=1, device_id=dev, device_id_type=MESH)
    pl.semaphore_wait(bar, 21)

    def a2a_copy(d):
        return rc(rows48(s_ref, col ^ d), rows48(ca, col), A2A + d, (row, col ^ d))

    yt = rc(tt_ref.at[1 - yh], tx.at[x, yh], YT, opp)
    yt.start()
    lax.fori_loop(1, 16, lambda d, n: (a2a_copy(d).start(), n)[1], 0)
    own_t = pltpu.make_async_copy(tt_ref.at[yh], tx.at[x, yh], lsem.at[0])
    own_t.start()
    own_s = pltpu.make_async_copy(rows48(s_ref, col), rows48(ca, col), lsem.at[1])
    own_s.start()
    own_l = pltpu.make_async_copy(l_ref, lx.at[core, z, yme], lsem.at[2])
    own_l.start()
    ydevs = [(row, ycol), (yrow, ycol), opp]
    ly = [rc(l_ref, lx.at[core, z, yme], LY + n, dev) for n, dev in enumerate(ydevs)]
    for copy in ly:
        copy.start()

    order = [(xo, 1 - yh), (xo, yh), (xm, 1 - yh), (xp, 1 - yh), (xp, yh), (xm, yh), (x, 1 - yh), (x, yh)]

    def w_copy(t):
        dx, dy = order[t]
        return pltpu.make_async_copy(w_ref.at[dy * 4 + dx], wbuf.at[t % 2], wsem.at[t % 2])

    w_copy(0).start()
    w_copy(1).start()

    def w_split(t):
        dx, dy = order[t]
        own = ml_ref[row]

        def step(a, carry):
            rows = pl.ds(pl.multiple_of(a * OT, OT), OT)
            labels = oi_ref[...] ^ virt_ref[(dy * 4 + dx) * VL + a]
            kept = jnp.where(labels == own, wbuf[t % 2, rows, :], 0.0)
            high, low = split2(kept)
            w_hi[rows, :] = high
            w_lo[rows, :] = low
            return carry

        lax.fori_loop(0, VL, step, 0)

    def w_mm(t):
        def step(n, carry):
            rows = pl.ds(pl.multiple_of(n * 256, 256), 256)
            high, low = w_hi[rows, :], w_lo[rows, :]
            part[t, rows, :] = dot(high, ca_hi[...]) + dot(high, ca_lo[...]) + dot(low, ca_hi[...])
            return carry

        lax.fori_loop(0, CK // 256, step, 0)

    def cyc(t):
        if t > 0:
            w_copy(t).wait()
            w_split(t)
            if t + 2 < 8:
                w_copy(t + 2).start()
        w_mm(t)

    def add_into(dst, src):
        def step(n, carry):
            rows = pl.ds(pl.multiple_of(n * 96, 96), 96)
            dst[rows, :] = dst[rows, :] + src[rows, :]
            return carry

        lax.fori_loop(0, CK // 96, step, 0)

    w_copy(0).wait()
    w_split(0)
    w_copy(2).start()

    own_t.wait()
    yt.wait_send()
    pltpu.make_async_remote_copy(
        src_ref=tt_ref.at[1 - yh], dst_ref=tx.at[x, 1 - yh], send_sem=ssem.at[YT], recv_sem=rsem.at[YT],
        device_id=opp, device_id_type=MESH,
    ).wait_recv()
    x1 = [rc(tx.at[x], tx.at[x], X1 + n, dev) for n, dev in enumerate((right, left))]
    for copy in x1:
        copy.start()

    own_s.wait()

    def a2a_wait(d, carry):
        a2a_copy(d).wait_send()
        rc(rows48(s_ref, col), rows48(ca, col ^ d), A2A + d, (row, col ^ d)).wait_recv()
        return carry

    lax.fori_loop(1, 16, a2a_wait, 0)

    def ca_step(n, carry):
        rows = pl.ds(pl.multiple_of(n * 256, 256), 256)
        high, low = split2(ca[...])
        ca_hi[rows, :] = dot(p_ref[rows, :], high).astype(BF16)
        ca_lo[rows, :] = dot(p_ref[rows, :], low).astype(BF16)
        return carry

    lax.fori_loop(0, CK // 256, ca_step, 0)

    rs = [
        rc(part.at[0], recv.at[0], RS + 0, right),
        rc(part.at[1], recv.at[1], RS + 1, left),
        rc(part.at[2], recv.at[2], RS + 2, left),
        rc(part.at[3], recv.at[3], RS + 3, right),
        rc(part.at[4], recv.at[4], RS + 4, right),
        rc(part.at[5], recv.at[5], RS + 5, left),
    ]
    cyc(0)
    rs[0].start()
    cyc(1)
    rs[1].start()

    own_l.wait()
    lyw = []
    for n, (dst_y) in enumerate((yh * 2 + 1 - yl, (1 - yh) * 2 + 1 - yl, (1 - yh) * 2 + yl)):
        ly[n].wait_send()
        rc(l_ref, lx.at[core, z, dst_y], LY + n, ydevs[n]).wait_recv()
    lz = [rc(lx.at[core, z], lx.at[core, z], LZ + n, dev) for n, dev in enumerate((up, down))]
    for copy in lz:
        copy.start()
    lc = [rc(lx.at[core, zz], lx.at[core, zz], LC + n, mate) for n, zz in enumerate((z, zm, zp, zo))]
    lc[0].start()

    cyc(2)
    rs[2].start()
    cyc(3)
    rs[0].wait_recv()
    add_into(part.at[3], recv.at[0])
    rs[3].start()
    cyc(4)
    rs[4].start()
    cyc(5)
    rs[1].wait_recv()
    add_into(part.at[5], recv.at[1])
    rs[5].start()

    rc(tx.at[xm], tx.at[xm], X1 + 0, left).wait_recv()
    rc(tx.at[xp], tx.at[xp], X1 + 1, right).wait_recv()
    x2 = [
        rc(tx.at[xm, 0], tx.at[xm, 0], X2 + 0, right),
        rc(tx.at[xp, 1], tx.at[xp, 1], X2 + 1, left),
    ]
    for copy in x2:
        copy.start()
    rc(lx.at[core, zm], lx.at[core, zm], LZ + 0, down).wait_recv()
    rc(lx.at[core, zp], lx.at[core, zp], LZ + 1, up).wait_recv()
    lz2 = [
        rc(lx.at[core, zm, pl.ds(0, 2)], lx.at[core, zm, pl.ds(0, 2)], LZ2 + 0, up),
        rc(lx.at[core, zp, pl.ds(2, 2)], lx.at[core, zp, pl.ds(2, 2)], LZ2 + 1, down),
    ]
    for copy in lz2:
        copy.start()
    lc[1].start()
    lc[2].start()

    cyc(6)
    cyc(7)

    rc(lx.at[core, zo, pl.ds(0, 2)], lx.at[core, zo, pl.ds(0, 2)], LZ2 + 0, down).wait_recv()
    rc(lx.at[core, zo, pl.ds(2, 2)], lx.at[core, zo, pl.ds(2, 2)], LZ2 + 1, up).wait_recv()
    lc[3].start()

    rs[3].wait_recv()
    rs[2].wait_recv()
    add_into(part.at[6], recv.at[3])
    add_into(part.at[6], recv.at[2])
    yr = rc(part.at[6], yrecv, YR, opp)
    yr.start()

    rc(tx.at[xo, 0], tx.at[xo, 0], X2 + 0, left).wait_recv()
    rc(tx.at[xo, 1], tx.at[xo, 1], X2 + 1, right).wait_recv()
    for n, zz in enumerate((z, zm, zp, zo)):
        rc(lx.at[1 - core, zz], lx.at[1 - core, zz], LC + n, mate).wait_recv()

    for h in range(2):
        oacc[h] = jnp.zeros((HIJ, AB), F32)

    def ladder(n, carry):
        kc, zz, yy = n // 16, (n // 4) % 4, n % 4
        cc = zz * 4 + (yy % 2) * 2 + kc
        h = yy // 2
        source = cc // 2

        def mask_step(a, inner):
            rows = pl.ds(pl.multiple_of(a * VT, VT), VT)
            labels = vb_ref[...] ^ virt_ref[(h * 4 + x) * VL + a]
            kept = jnp.where(labels == vl_ref[cc], lx[kc, zz, yy, rows, :], 0.0)
            high, low = split2(kept)
            l_hi[rows, :] = high
            l_lo[rows, :] = low
            return inner

        lax.fori_loop(0, VL, mask_step, 0)
        lanes = pl.ds(pl.multiple_of(kc * CD, CD), CD)
        t_hi, t_lo = split2(tx[source % 4, source // 4, :, lanes])
        oacc[h] = oacc[h] + (dot_nt(t_hi, l_hi[...]) + dot_nt(t_lo, l_hi[...]) + dot_nt(t_hi, l_lo[...]))
        return carry

    lax.fori_loop(0, 32, ladder, 0)
    out_own = pltpu.make_async_copy(oacc.at[yh], lo_ref.at[yh], lsem.at[0])
    out_own.start()
    ob = rc(oacc.at[1 - yh], lo_ref.at[yh], OB, opp)
    ob.start()

    rs[4].wait_recv()
    rs[5].wait_recv()
    add_into(part.at[7], recv.at[4])
    add_into(part.at[7], recv.at[5])
    yr.wait_recv()
    add_into(part.at[7], yrecv)

    def back_step(n, carry):
        rows = pl.ds(pl.multiple_of(n * 256, 256), 256)
        value = part[7]
        high, low = split2(value)
        rest = (value - high.astype(F32) - low.astype(F32)).astype(BF16)
        sel = q_ref[rows, :]
        cp[rows, :] = dot(sel, high) + dot(sel, low) + dot(sel, rest)
        return carry

    lax.fori_loop(0, CK // 256, back_step, 0)

    def back_copy(d):
        return rc(rows48(cp, col ^ d), rows48(d_ref, col), BACK + d, (row, col ^ d))

    lax.fori_loop(1, 16, lambda d, n: (back_copy(d).start(), n)[1], 0)
    own_d = pltpu.make_async_copy(rows48(cp, col), rows48(d_ref, col), lsem.at[1])
    own_d.start()

    for copy in x1 + x2 + lz + lz2 + lc + rs + [yr, ob]:
        copy.wait_send()
    rc(oacc.at[yh], lo_ref.at[1 - yh], OB, opp).wait_recv()
    out_own.wait()
    own_d.wait()

    def back_wait(d, carry):
        back_copy(d).wait_send()
        rc(rows48(cp, col), rows48(d_ref, col ^ d), BACK + d, (row, col ^ d)).wait_recv()
        return carry

    lax.fori_loop(1, 16, back_wait, 0)


def permutation():
    a, c, i = np.meshgrid(np.arange(VL), np.arange(16), np.arange(OL), indexing="ij")
    table = np.zeros((CK, CK), np.float32)
    table[(a * OT + c * OL + i).reshape(-1), (c * BLK + a * OL + i).reshape(-1)] = 1.0
    return table


def body(amps, ladder_ints, cycle_ints, virt_irrep, occ_irrep, virt_energy, occ_energy):
    row, col = lax.axis_index("row"), lax.axis_index("col")
    sent = amps.reshape(VL, 16, VC, OL, OT).transpose(1, 0, 3, 2, 4).reshape(CK, BJ)
    turned = amps.T.reshape(2, HIJ, AB)
    mixed = (virt_irrep[:, None] ^ occ_irrep[None, :]).reshape(8, 1, CK)
    pairs = (virt_irrep[:, None] ^ virt_irrep[None, :]).reshape(16, 1, CD)
    table = permutation()
    forward = jnp.asarray(table, BF16)
    backward = jnp.asarray(table.T, BF16)
    anywhere = pl.BlockSpec(memory_space=pl.ANY)
    vmem = pl.BlockSpec(memory_space=pltpu.VMEM)
    ladder, cycle = pl.pallas_call(
        kernel,
        out_shape=(
            jax.ShapeDtypeStruct((2, HIJ, AB), F32),
            jax.ShapeDtypeStruct((CK, BJ), F32),
        ),
        in_specs=[pl.BlockSpec(memory_space=pltpu.SMEM)] + [anywhere] * 4 + [vmem] * 6,
        out_specs=(anywhere, anywhere),
        scratch_shapes=[
            pltpu.VMEM((4, 2, HIJ, AB), F32),
            pltpu.VMEM((2, 4, 4, AB, CD), F32),
            pltpu.VMEM((CK, BJ), F32),
            pltpu.VMEM((CK, BJ), BF16),
            pltpu.VMEM((CK, BJ), BF16),
            pltpu.VMEM((2, CK, CK), F32),
            pltpu.VMEM((CK, CK), BF16),
            pltpu.VMEM((CK, CK), BF16),
            pltpu.VMEM((8, CK, BJ), F32),
            pltpu.VMEM((6, CK, BJ), F32),
            pltpu.VMEM((CK, BJ), F32),
            pltpu.VMEM((2, HIJ, AB), F32),
            pltpu.VMEM((AB, CD), BF16),
            pltpu.VMEM((AB, CD), BF16),
            pltpu.VMEM((CK, BJ), F32),
            pltpu.SemaphoreType.DMA((NSEM,)),
            pltpu.SemaphoreType.DMA((NSEM,)),
            pltpu.SemaphoreType.DMA((2,)),
            pltpu.SemaphoreType.DMA((3,)),
        ],
        compiler_params=pltpu.CompilerParams(
            collective_id=0, has_side_effects=True, vmem_limit_bytes=67043328
        ),
    )(
        virt_irrep, sent, turned, ladder_ints, cycle_ints.reshape(8, CK, CK), mixed, pairs,
        occ_irrep.reshape(OT, 1), virt_irrep.reshape(VT, 1), forward, backward,
    )
    back = cycle.reshape(16, VL, OL, VC, OT).transpose(1, 0, 3, 2, 4).reshape(AB, OL * OT)
    own_virt = lax.dynamic_slice_in_dim(virt_energy, row * VL, VL)
    own_occ = lax.dynamic_slice_in_dim(occ_energy, col * OL, OL)
    row_energy = (own_virt[:, None] + virt_energy[None, :]).reshape(-1)
    col_energy = (own_occ[:, None] + occ_energy[None, :]).reshape(-1)
    return (ladder.reshape(OL * OT, AB).T + back) / (row_energy[:, None] - col_energy[None, :])


def solution(mesh):
    placed = (P("row", "col"), P("row", "col"), P(None, "row"), P(), P(), P(), P())
    return jax.shard_map(
        body, mesh=mesh, in_specs=placed, out_specs=P("row", "col"), check_vma=False
    )
```

time: 342 us -> 227 us (0.66)
  waiting for transfers between devices: 244 us -> 0 us
  Pallas kernels: 0 us -> 203 us
  matrix products: 54.9 us -> 0 us
  between operations: 15 us -> 0.13 us
  starting transfers between devices: 12.6 us -> 0 us
  local copies, waits for them, and re-layouts: 15.3 us -> 19 us
    pallas_call x0 -> x1, Pallas kernels: none -> 203 us  [body(): pl.pallas_call(kernel, out_shape=(jax.ShapeDtypeStruct((2, HIJ, AB), F32)...]
    reduce_scatter x1 -> x0, waiting for transfers between devices: 150 us -> none  [body(): lax.psum_scatter(jnp.dot(part, cycle_amps, precision=highest, preferred_e...]
    all_to_all x2 -> x0, waiting for transfers between devices: 58.7 us -> none  [the longest x1 36.9 us: body(): lax.all_to_all(cycle_blocks, 'col', split_axis=1, concat_axis=2, tiled=True)]
    dot_general x2 -> x0, matrix products: 54.9 us -> none  [the longest x1 35.1 us: body(): jnp.dot(part, cycle_amps, precision=highest, preferred_element_type=jnp.f...]
    all_gather x2 -> x0, waiting for transfers between devices: 34.2 us -> none  [the longest x1 34.2 us: body(): lax.all_gather(amps, 'row', axis=0, tiled=True)]
    all_to_all x2 -> x0, starting transfers between devices: 12.4 us -> none  [the longest x1 6.67 us: body(): lax.all_to_all(blocks, 'col', split_axis=1, concat_axis=2, tiled=True)]
  transfers between devices with their start and end apart: 5 -> 0, of which waited for: 4 -> 0; matrix products, arithmetic and copies ran while one was open for 3% -> 0% of each run, Pallas kernels for 0% -> 0%
where the time goes in v1:
time: 227 us; the launch traced here: 225 us
  Pallas kernels  203 us (89%)
  local copies, waits for them, and re-layouts  19 us (8%)
  other arithmetic  2.71 us (1%)
    pallas_call x1, Pallas kernels, body(): pl.pallas_call(kernel, out_shape=(jax.ShapeDtypeStruct((2, HIJ, AB), F32)...  203 us
    reshape x3, local copies, waits for them, and re-layouts, body(): cycle.reshape(16, VL, OL, VC, OT).transpose(1, 0, 3, 2, 4)  5.36 us

profile of v1, /device:TPU:0, one launch (start us, length us, event | category | flops | bytes accessed | tf_op | source)
XLA Modules:
  0.0 225.1 jit_solution(14929446419544648205)
XLA Ops:
  0.0 1.7 copy.14
  1.7 0.7 reshape.139
  2.3 1.6 copy.15
  3.9 2.9 %reshape.140.s_ref = f32[768,384]{1,0:T(8,128)} reshape(f32[16,8,6,4,96]{4,3,2,1,0:T(4,128)} %copy.15) | data formatting | bytes 2359296 | tf_op jit(solution)/shard_map/reshape | solution.py:333
  6.8 0.0 copy-done
  6.8 0.1 xor.56
  6.9 0.1 xor.57
  7.0 0.1 xor.58
  7.1 0.1 xor.60
  7.2 0.6 broadcast_xor_fusion.ml_ref
  7.8 0.1 xor.63
  7.9 0.1 xor.64
  8.0 0.1 xor.65
  8.1 0.1 xor.67
  8.2 0.6 broadcast_xor_fusion.1.vl_ref
  8.8 0.7 copy.16.oi_ref
  9.5 0.7 copy.17.vb_ref
  10.2 203.3 %shard_map.91 = (f32[2,288,512]{2,1,0:T(8,128)}, f32[768,384]{1,0:T(8,128)}) custom-call(s32[64]{0:T(128)} %virt_ref.1, f32[768,384]{1,0:T(8,128)} %reshape.140.s_ref, f32[2,288,512]{2,1,0:T(8,128)} %bitcast.18, f32[512,256]{1,0:T(8,128)} %l_ref.1, f32[8,768,768]{2,1,0:T(8,128)} %bitcast.15, s32[8,1,768]{2,1,0:T(1,128)} %broadcast_xor_fusion.ml_ref, ...), custom_call_target="tpu_custom_call" | custom-call | tf_op jit(solution)/shard_map/pallas_call | solution.py:342
  213.5 3.1 %reshape.145 = f32[16,8,6,4,96]{4,3,2,1,0:T(4,128)} reshape(f32[768,384]{1,0:T(8,128)} %get-tuple-element.8) | data formatting | bytes 2359296 | tf_op jit(solution)/shard_map/reshape | solution.py:378
  216.6 1.7 copy.22
  218.3 0.5 reshape.146
  218.9 0.0 copy-start.2
  218.9 0.0 copy-start.3
  218.9 1.7 copy.18
  220.6 0.1 dynamic_slice.7
  220.7 0.1 broadcast_add_fusion
  220.7 0.1 add.59
  220.8 0.1 dynamic_slice.6
  220.9 0.1 broadcast_add_fusion.1
  221.0 0.1 add.54
  221.0 1.3 fusion
  222.4 2.7 %copy.20 = f32[512,576]{0,1:T(8,128)} copy(f32[512,576]{1,0:T(8,128)} %fusion) | data formatting | bytes 2359296 | tf_op jit(solution)/shard_map/div | solution.py:383
  (7 shorter events, 0.0 us)
Async XLA Ops:
  3.9 2.9 %copy-start = (s32[64]{0:T(128)S(1)}, s32[64]{0:T(128)}, u32[]{:S(2)}) copy-start(s32[64]{0:T(128)} %virt_ref.1) | copy-start | bytes 772
  3.9 3.2 %copy-start.1 = (s32[96]{0:T(128)S(1)}, s32[96]{0:T(128)}, u32[]{:S(2)}) copy-start(s32[96]{0:T(128)} %param.13) | copy-start | bytes 1156
  218.9 1.7 copy-start.2
  218.9 1.9 copy-start.3

commit v2 on v1

v2 whole, which is shorter than its diff:
```python
import functools

import jax
import jax.numpy as jnp
import numpy as np
from jax import lax
from jax.experimental import pallas as pl
from jax.experimental.pallas import tpu as pltpu
from jax.sharding import PartitionSpec as P

MESH = pl.DeviceIdType.MESH
F32, BF16 = jnp.float32, jnp.bfloat16

VT, OT = 64, 96
VL, OL, VC = 8, 6, 4
CK = VL * OT
BJ = VC * OT
HALF = CK // 2
BLK = VL * OL // 2
AB = VL * VT
CD = 256
HIJ = OL * OT // 2

A2A, BACK = 0, 16
YT, X1, X2, LY, LZ, LZ2, LC, OB = 32, 33, 37, 39, 42, 50, 52, 56
RS, YR, BACK2 = 57, 65, 66
NSEM = 83


def split2(value):
    high = value.astype(BF16)
    low = (value - high.astype(F32)).astype(BF16)
    return high, low


def dot(a, b):
    return jnp.dot(a, b, preferred_element_type=F32)


def kernel(
    virt_ref, s_ref, tt_ref, l_ref, w_ref, virt_lanes, occ_lanes, p_ref, q_ref,
    lo_ref, d_ref,
    tx, lx, ca, ca_hi, ca_lo, wbuf, w_hi, w_lo, part, recv, yrecv, oacc, lmask, cp, ml_ref, vl_ref, oi_ref, vb_ref,
    ssem, rsem, wsem, lsem,
):
    row, col = lax.axis_index("row"), lax.axis_index("col")
    yh, x = row // 4, row % 4
    z, yl, core = col // 4, (col // 2) % 2, col % 2
    yme = yh * 2 + yl
    xp, xm, xo = (x + 1) % 4, (x + 3) % 4, (x + 2) % 4
    zp, zm, zo = (z + 1) % 4, (z + 3) % 4, (z + 2) % 4
    right, left = (yh * 4 + xp, col), (yh * 4 + xm, col)
    up, down = (row, zp * 4 + col % 4), (row, zm * 4 + col % 4)
    yrow = (1 - yh) * 4 + x
    ycol = z * 4 + (1 - yl) * 2 + core
    opp = (yrow, col)
    mate = (row, z * 4 + yl * 2 + (1 - core))

    def rc(src, dst, k, dev):
        return pltpu.make_async_remote_copy(
            src_ref=src, dst_ref=dst, send_sem=ssem.at[k], recv_sem=rsem.at[k],
            device_id=dev, device_id_type=MESH,
        )

    def upright(lanes, count):
        spread = jnp.broadcast_to(lanes, (count, count))
        at = lax.broadcasted_iota(jnp.int32, (count, count), 0) == lax.broadcasted_iota(jnp.int32, (count, count), 1)
        return jnp.sum(jnp.where(at, spread, 0), axis=1, keepdims=True)

    oi_ref[...] = upright(occ_lanes[...], OT)
    vb_ref[...] = upright(virt_lanes[...], VT)
    for a in range(VL):
        ml_ref[:, a * OT : (a + 1) * OT] = occ_lanes[...] ^ virt_ref[row * VL + a]
    for a in range(VC):
        vl_ref[:, a * VT : (a + 1) * VT] = virt_lanes[...] ^ virt_ref[col * VC + a]

    def l_step(a, carry):
        rows = pl.ds(pl.multiple_of(a * VT, VT), VT)
        labels = vb_ref[...] ^ virt_ref[row * VL + a]
        lmask[rows, :] = jnp.where(labels == vl_ref[...], l_ref[rows, :], 0.0)
        return carry

    lax.fori_loop(0, VL, l_step, 0)
    lx[core, z, yme] = lmask[...].T

    bar = pltpu.get_barrier_semaphore()

    def greet(d, carry):
        pl.semaphore_signal(bar, inc=1, device_id=(row, col ^ d), device_id_type=MESH)
        return carry

    lax.fori_loop(1, 16, greet, 0)
    for dev in (right, left, up, down, opp, (yrow, ycol)):
        pl.semaphore_signal(bar, inc=1, device_id=dev, device_id_type=MESH)
    pl.semaphore_wait(bar, 21)

    def a2a_copy(d):
        return rc(s_ref.at[:, col ^ d], ca.at[:, col], A2A + d, (row, col ^ d))

    yt = rc(tt_ref.at[1 - yh], tx.at[x, yh], YT, opp)
    yt.start()
    x1 = [rc(tt_ref.at[yh], tx.at[x, yh], X1 + n, dev) for n, dev in enumerate((right, left))]
    for copy in x1:
        copy.start()
    lax.fori_loop(1, 16, lambda d, n: (a2a_copy(d).start(), n)[1], 0)
    own_t = pltpu.make_async_copy(tt_ref.at[yh], tx.at[x, yh], lsem.at[0])
    own_t.start()
    own_s = pltpu.make_async_copy(s_ref.at[:, col], ca.at[:, col], lsem.at[1])
    own_s.start()
    own_l = lx.at[core, z, yme]
    ydevs = [(row, ycol), (yrow, ycol), opp]
    yidx = [yh * 2 + 1 - yl, (1 - yh) * 2 + 1 - yl, (1 - yh) * 2 + yl]
    ly = [rc(own_l, own_l, LY + n, dev) for n, dev in enumerate(ydevs)]
    for copy in ly:
        copy.start()
    lz = [rc(own_l, own_l, LZ + n, dev) for n, dev in enumerate((up, down))]
    for copy in lz:
        copy.start()

    order = [(xo, 1 - yh), (xo, yh), (xm, 1 - yh), (xp, 1 - yh), (xp, yh), (xm, yh), (x, 1 - yh), (x, yh)]

    def w_copy(t):
        dx, dy = order[t]
        return pltpu.make_async_copy(w_ref.at[dy * 4 + dx], wbuf.at[t % 2], wsem.at[t % 2])

    w_copy(0).start()
    w_copy(1).start()

    def w_split(t):
        dx, dy = order[t]
        own = ml_ref[...]

        def step(a, carry):
            rows = pl.ds(pl.multiple_of(a * OT, OT), OT)
            labels = oi_ref[...] ^ virt_ref[(dy * 4 + dx) * VL + a]
            kept = jnp.where(labels == own, wbuf[t % 2, rows, :], 0.0)
            high, low = split2(kept)
            w_hi[rows, :] = high
            w_lo[rows, :] = low
            return carry

        lax.fori_loop(0, VL, step, 0)

    def w_mm(t):
        def step(n, carry):
            rows = pl.ds(pl.multiple_of(n * 256, 256), 256)
            high, low = w_hi[rows, :], w_lo[rows, :]
            part[t, rows, :] = dot(high, ca_hi[...]) + dot(high, ca_lo[...]) + dot(low, ca_hi[...])
            return carry

        lax.fori_loop(0, CK // 256, step, 0)

    def cyc(t):
        if t > 0:
            w_copy(t).wait()
            w_split(t)
            if t + 2 < 8:
                w_copy(t + 2).start()
        w_mm(t)

    def add_into(dst, src):
        def step(n, carry):
            rows = pl.ds(pl.multiple_of(n * 96, 96), 96)
            dst[rows, :] = dst[rows, :] + src[rows, :]
            return carry

        lax.fori_loop(0, CK // 96, step, 0)

    w_copy(0).wait()
    w_split(0)
    w_copy(2).start()

    own_t.wait()
    yt.wait_send()
    pltpu.make_async_remote_copy(
        src_ref=tt_ref.at[1 - yh], dst_ref=tx.at[x, 1 - yh], send_sem=ssem.at[YT], recv_sem=rsem.at[YT],
        device_id=opp, device_id_type=MESH,
    ).wait_recv()
    x1b = [rc(tx.at[x, 1 - yh], tx.at[x, 1 - yh], X1 + 2 + n, dev) for n, dev in enumerate((right, left))]
    for copy in x1b:
        copy.start()

    own_s.wait()

    def a2a_wait(d, carry):
        a2a_copy(d).wait_send()
        rc(s_ref.at[:, col], ca.at[:, col ^ d], A2A + d, (row, col ^ d)).wait_recv()
        return carry

    lax.fori_loop(1, 16, a2a_wait, 0)

    for half in range(2):
        high, low = split2(ca[half].reshape(HALF, BJ))
        rows = pl.ds(half * HALF, HALF)
        ca_hi[rows, :] = dot(p_ref[...], high).astype(BF16)
        ca_lo[rows, :] = dot(p_ref[...], low).astype(BF16)

    rs = [
        rc(part.at[0], recv.at[0], RS + 0, right),
        rc(part.at[1], recv.at[1], RS + 1, left),
        rc(part.at[2], recv.at[2], RS + 2, left),
        rc(part.at[3], recv.at[3], RS + 3, right),
    ]
    halves = [pl.ds(0, HALF), pl.ds(HALF, HALF)]
    rs4 = [rc(part.at[4, rows], recv.at[4, rows], RS + 4 + n, right) for n, rows in enumerate(halves)]
    rs5 = [rc(part.at[5, rows], recv.at[5, rows], RS + 6 + n, left) for n, rows in enumerate(halves)]
    cyc(0)
    rs[0].start()
    cyc(1)
    rs[1].start()

    for n, dst_y in enumerate(yidx):
        ly[n].wait_send()
        block = lx.at[core, z, dst_y]
        rc(own_l, block, LY + n, ydevs[n]).wait_recv()
        for m, dev in enumerate((up, down)):
            copy = rc(block, block, LZ + 2 + 2 * n + m, dev)
            copy.start()
            lz.append(copy)
    lc = [rc(lx.at[core, zz], lx.at[core, zz], LC + n, mate) for n, zz in enumerate((z, zm, zp, zo))]
    lc[0].start()

    cyc(2)
    rs[2].start()
    cyc(3)
    rs[0].wait_recv()
    add_into(part.at[3], recv.at[0])
    rs[3].start()
    cyc(4)
    rs4[0].start()
    rs4[1].start()
    cyc(5)
    rs[1].wait_recv()
    add_into(part.at[5], recv.at[1])
    rs5[0].start()
    rs5[1].start()

    for h, base in ((yh, X1), (1 - yh, X1 + 2)):
        rc(tx.at[xm, h], tx.at[xm, h], base, left).wait_recv()
        rc(tx.at[xp, h], tx.at[xp, h], base + 1, right).wait_recv()
    x2 = [
        rc(tx.at[xm, 0], tx.at[xm, 0], X2 + 0, right),
        rc(tx.at[xp, 1], tx.at[xp, 1], X2 + 1, left),
    ]
    for copy in x2:
        copy.start()
    for n, src_y in enumerate([yme] + yidx):
        rc(lx.at[core, zm, src_y], lx.at[core, zm, src_y], LZ + 2 * n, down).wait_recv()
        rc(lx.at[core, zp, src_y], lx.at[core, zp, src_y], LZ + 2 * n + 1, up).wait_recv()
    lz2 = [
        rc(lx.at[core, zm, pl.ds(0, 2)], lx.at[core, zm, pl.ds(0, 2)], LZ2 + 0, up),
        rc(lx.at[core, zp, pl.ds(2, 2)], lx.at[core, zp, pl.ds(2, 2)], LZ2 + 1, down),
    ]
    for copy in lz2:
        copy.start()
    lc[1].start()
    lc[2].start()

    cyc(6)
    cyc(7)

    rs[3].wait_recv()
    rs[2].wait_recv()
    add_into(part.at[6], recv.at[3])
    add_into(part.at[6], recv.at[2])
    yr = [rc(part.at[6, rows], yrecv.at[rows], YR + 17 * n, opp) for n, rows in enumerate(halves)]
    for copy in yr:
        copy.start()

    rc(lx.at[core, zo, pl.ds(0, 2)], lx.at[core, zo, pl.ds(0, 2)], LZ2 + 0, down).wait_recv()
    rc(lx.at[core, zo, pl.ds(2, 2)], lx.at[core, zo, pl.ds(2, 2)], LZ2 + 1, up).wait_recv()
    lc[3].start()
    for n, zz in enumerate((z, zm, zp, zo)):
        rc(lx.at[1 - core, zz], lx.at[1 - core, zz], LC + n, mate).wait_recv()

    for h in range(2):
        oacc[h] = jnp.zeros((HIJ, AB), F32)

    def ladder(sx, n):
        kc, sy = n // 2, n % 2
        source = sy * 4 + sx
        zz, ylo = source // 2, source % 2
        lanes = pl.ds(pl.multiple_of(kc * CD, CD), CD)
        t_hi, t_lo = split2(tx[sx, sy, :, lanes])
        both = jnp.concatenate([t_hi, t_lo], axis=0)
        for h in range(2):
            high, low = split2(lx[kc, zz, h * 2 + ylo])
            wide = dot(both, high)
            oacc[h] = oacc[h] + (wide[:HIJ] + wide[HIJ:] + dot(t_hi, low))

    lax.fori_loop(0, 12, lambda n, carry: (ladder((x + 3 + n // 4) % 4, n % 4), carry)[1], 0)

    def back_copy(n, base, d):
        return rc(cp.at[n, col ^ d], d_ref.at[n, col], base + d, (row, col ^ d))

    own_d = [pltpu.make_async_copy(cp.at[n, col], d_ref.at[n, col], lsem.at[1 + n]) for n in range(2)]
    for n, base in ((0, BACK), (1, BACK2)):
        rows = halves[n]
        rs4[n].wait_recv()
        rs5[n].wait_recv()
        rc(part.at[6, rows], yrecv.at[rows], YR + 17 * n, opp).wait_recv()
        value = (part[7, rows, :] + recv[4, rows, :]) + (recv[5, rows, :] + yrecv[rows, :])
        high, low = split2(value)
        rest = (value - high.astype(F32) - low.astype(F32)).astype(BF16)
        sel = q_ref[...]
        cp[n] = (dot(sel, high) + dot(sel, low) + dot(sel, rest)).reshape(16, BLK, BJ)
        lax.fori_loop(1, 16, lambda d, carry: (back_copy(n, base, d).start(), carry)[1], 0)
        own_d[n].start()

    rc(tx.at[xo, 0], tx.at[xo, 0], X2 + 0, left).wait_recv()
    rc(tx.at[xo, 1], tx.at[xo, 1], X2 + 1, right).wait_recv()
    lax.fori_loop(0, 4, lambda n, carry: (ladder(xo, n), carry)[1], 0)
    out_own = pltpu.make_async_copy(oacc.at[yh], lo_ref.at[yh], lsem.at[0])
    out_own.start()
    ob = rc(oacc.at[1 - yh], lo_ref.at[yh], OB, opp)
    ob.start()

    for copy in x1 + x1b + x2 + lz + lz2 + lc + rs + rs4 + rs5 + yr + [ob]:
        copy.wait_send()
    rc(oacc.at[yh], lo_ref.at[1 - yh], OB, opp).wait_recv()
    out_own.wait()
    for n, base in ((0, BACK), (1, BACK2)):
        own_d[n].wait()

        def back_wait(d, carry):
            back_copy(n, base, d).wait_send()
            rc(cp.at[n, col], d_ref.at[n, col ^ d], base + d, (row, col ^ d)).wait_recv()
            return carry

        lax.fori_loop(1, 16, back_wait, 0)


def permutation():
    a, c, i = np.meshgrid(np.arange(VL // 2), np.arange(16), np.arange(OL), indexing="ij")
    table = np.zeros((HALF, HALF), np.float32)
    table[(a * OT + c * OL + i).reshape(-1), (c * BLK + a * OL + i).reshape(-1)] = 1.0
    return table


def body(amps, ladder_ints, cycle_ints, virt_irrep, occ_irrep, virt_energy, occ_energy):
    row, col = lax.axis_index("row"), lax.axis_index("col")
    sent = amps.reshape(2, VL // 2, 16, VC, OL, OT).transpose(0, 2, 1, 4, 3, 5).reshape(2, 16, BLK, BJ)
    turned = amps.T.reshape(2, HIJ, AB)
    table = permutation()
    forward = jnp.asarray(table, BF16)
    backward = jnp.asarray(table.T, BF16)
    anywhere = pl.BlockSpec(memory_space=pl.ANY)
    vmem = pl.BlockSpec(memory_space=pltpu.VMEM)
    ladder, cycle = pl.pallas_call(
        kernel,
        out_shape=(
            jax.ShapeDtypeStruct((2, HIJ, AB), F32),
            jax.ShapeDtypeStruct((2, 16, BLK, BJ), F32),
        ),
        in_specs=[pl.BlockSpec(memory_space=pltpu.SMEM)] + [anywhere] * 2 + [vmem, anywhere] + [vmem] * 4,
        out_specs=(anywhere, anywhere),
        scratch_shapes=[
            pltpu.VMEM((4, 2, HIJ, AB), F32),
            pltpu.VMEM((2, 4, 4, CD, AB), F32),
            pltpu.VMEM((2, 16, BLK, BJ), F32),
            pltpu.VMEM((CK, BJ), BF16),
            pltpu.VMEM((CK, BJ), BF16),
            pltpu.VMEM((2, CK, CK), F32),
            pltpu.VMEM((CK, CK), BF16),
            pltpu.VMEM((CK, CK), BF16),
            pltpu.VMEM((8, CK, BJ), F32),
            pltpu.VMEM((6, CK, BJ), F32),
            pltpu.VMEM((CK, BJ), F32),
            pltpu.VMEM((2, HIJ, AB), F32),
            pltpu.VMEM((AB, CD), F32),
            pltpu.VMEM((2, 16, BLK, BJ), F32),
            pltpu.VMEM((1, CK), jnp.int32),
            pltpu.VMEM((1, CD), jnp.int32),
            pltpu.VMEM((OT, 1), jnp.int32),
            pltpu.VMEM((VT, 1), jnp.int32),
            pltpu.SemaphoreType.DMA((NSEM,)),
            pltpu.SemaphoreType.DMA((NSEM,)),
            pltpu.SemaphoreType.DMA((2,)),
            pltpu.SemaphoreType.DMA((3,)),
        ],
        compiler_params=pltpu.CompilerParams(
            collective_id=0, has_side_effects=True, vmem_limit_bytes=67043328
        ),
    )(
        virt_irrep, sent, turned, ladder_ints, cycle_ints.reshape(8, CK, CK),
        virt_irrep.reshape(1, VT), occ_irrep.reshape(1, OT), forward, backward,
    )
    back = cycle.reshape(2, 16, VL // 2, OL, VC, OT).transpose(3, 5, 0, 2, 1, 4).reshape(OL * OT, AB)
    own_virt = lax.dynamic_slice_in_dim(virt_energy, row * VL, VL)
    own_occ = lax.dynamic_slice_in_dim(occ_energy, col * OL, OL)
    row_energy = (own_virt[:, None] + virt_energy[None, :]).reshape(-1)
    col_energy = (own_occ[:, None] + occ_energy[None, :]).reshape(-1)
    return ((ladder.reshape(OL * OT, AB) + back) / (row_energy[None, :] - col_energy[:, None])).T


def solution(mesh):
    placed = (P("row", "col"), P("row", "col"), P(None, "row"), P(), P(), P(), P())
    return jax.shard_map(
        body, mesh=mesh, in_specs=placed, out_specs=P("row", "col"), check_vma=False
    )
```

time: 227 us -> 177 us (0.78)
  Pallas kernels: 203 us -> 154 us
    pallas_call x1, Pallas kernels: 203 us -> 154 us  [body(): pl.pallas_call(kernel, out_shape=(jax.ShapeDtypeStruct((2, HIJ, AB), F32)...]
    div x1 -> x0, local copies, waits for them, and re-layouts: 2.71 us -> none  [body(): (ladder.reshape(OL * OT, AB).T + back) / (row_energy[:, None] - col_energ...]
    transpose x1 -> x2, local copies, waits for them, and re-layouts: 1.59 us -> 4.29 us  [the longest x1 2.71 us: body(): return ((ladder.reshape(OL * OT, AB) + back) / (row_energy[None, :] - col...]
    reshape x7 -> x6, local copies, waits for them, and re-layouts: 11.3 us -> 10.8 us  [the longest x3 5.56 us: body(): cycle.reshape(2, 16, VL // 2, OL, VC, OT).transpose(3, 5, 0, 2, 1, 4)]
where the time goes in v2:
time: 177 us; the launch traced here: 176 us
  Pallas kernels  154 us (87%)
  local copies, waits for them, and re-layouts  19.5 us (11%)
  other arithmetic  2.76 us (2%)
    pallas_call x1, Pallas kernels, body(): pl.pallas_call(kernel, out_shape=(jax.ShapeDtypeStruct((2, HIJ, AB), F32)...  154 us
    reshape x3, local copies, waits for them, and re-layouts, body(): cycle.reshape(2, 16, VL // 2, OL, VC, OT).transpose(3, 5, 0, 2, 1, 4)  5.56 us

profile of v2, /device:TPU:0, one launch (start us, length us, event | category | flops | bytes accessed | tf_op | source)
XLA Modules:
  0.0 176.2 jit_solution(6837806205142137708)
XLA Ops:
  0.0 0.7 dynamic_slice.7
  0.7 0.7 broadcast_add_fusion
  1.5 0.7 add.59
  2.1 0.7 dynamic_slice.6
  2.8 0.7 broadcast_add_fusion.1
  3.6 0.7 add.54
  4.2 1.7 copy.12
  5.9 0.7 reshape.59
  6.6 1.6 copy.13
  8.1 2.9 %reshape.60.s_ref = f32[2,16,24,384]{3,2,1,0:T(8,128)} reshape(f32[2,16,4,6,4,96]{5,4,3,2,1,0:T(4,128)} %copy.13) | data formatting | bytes 2359296 | tf_op jit(solution)/shard_map/reshape | solution.py:342
  11.0 153.9 %shard_map.91 = (f32[2,288,512]{2,1,0:T(8,128)}, f32[2,16,24,384]{3,2,1,0:T(8,128)}) custom-call(s32[64]{0:T(128)} %virt_ref.1, f32[2,16,24,384]{3,2,1,0:T(8,128)} %reshape.60.s_ref, f32[2,288,512]{2,1,0:T(8,128)} %bitcast.20, f32[512,256]{1,0:T(8,128)} %l_ref.1, f32[8,768,768]{2,1,0:T(8,128)} %bitcast.17, s32[1,64]{1,0:T(1,128)} %bitcast.22, ...), custom_call_target="tpu_custom_call" | custom-call | tf_op jit(solution)/shard_map/pallas_call | solution.py:349
  164.9 3.3 %reshape.66 = f32[2,16,4,6,4,96]{5,4,3,2,1,0:T(4,128)} reshape(f32[2,16,24,384]{3,2,1,0:T(8,128)} %get-tuple-element.8) | data formatting | bytes 2359296 | tf_op jit(solution)/shard_map/reshape | solution.py:388
  168.2 1.8 copy.18
  170.0 0.5 reshape.67
  170.5 0.0 copy-start
  170.5 0.0 copy-start.1
  170.5 1.7 copy.15
  172.2 0.0 copy-done
  172.2 0.0 copy-done.1
  172.2 1.3 divide_bitcast_fusion
  173.5 2.7 %copy.16 = f32[512,576]{0,1:T(8,128)} copy(f32[512,576]{1,0:T(8,128)} %divide_bitcast_fusion) | data formatting | bytes 2359296 | tf_op jit(solution)/shard_map/transpose | solution.py:393
Async XLA Ops:
  170.5 1.7 copy-start
  170.5 1.7 copy-start.1

commit v3 on v2

v3 whole, which is shorter than its diff:
```python
import functools

import jax
import jax.numpy as jnp
import numpy as np
from jax import lax
from jax.experimental import pallas as pl
from jax.experimental.pallas import tpu as pltpu
from jax.sharding import PartitionSpec as P

MESH = pl.DeviceIdType.MESH
F32, BF16 = jnp.float32, jnp.bfloat16

VT, OT = 64, 96
VL, OL, VC = 8, 6, 4
CK = VL * OT
BJ = VC * OT
BLK = VL * OL
THIRD = BJ // 3
AB = VL * VT
CD = 256
HIJ = OL * OT // 2

A2A, BACK, YT, X1, X2, LY = 0, 16, 64, 65, 69, 73
LZ, LZ2, LC, OB, RS, YR = 76, 84, 86, 90, 91, 105
NSEM = 108


def split2(value):
    high = value.astype(BF16)
    low = (value - high.astype(F32)).astype(BF16)
    return high, low


def dot_nt(a, b):
    return lax.dot_general(a, b, (((1,), (1,)), ((), ())), preferred_element_type=F32)


def dot(a, b):
    return jnp.dot(a, b, preferred_element_type=F32)


def kernel(
    virt_ref, ve_ref, oe_ref, tt_ref, l_ref, w_ref, virt_lanes, occ_lanes, ve_lanes, oe_lanes, p_ref, q_ref,
    lo_ref, d_ref, row_e, col_e,
    tt, s_ref, tx, lx, raw, ca, ca_hi, ca_lo, wbuf, w_hi, w_lo, part, recv, yrecv, oacc, lmask, cp, ml_ref, vl_ref, oi_ref, vb_ref,
    ssem, rsem, wsem, lsem,
):
    row, col = lax.axis_index("row"), lax.axis_index("col")
    yh, x = row // 4, row % 4
    z, yl, core = col // 4, (col // 2) % 2, col % 2
    yme = yh * 2 + yl
    xp, xm, xo = (x + 1) % 4, (x + 3) % 4, (x + 2) % 4
    zp, zm, zo = (z + 1) % 4, (z + 3) % 4, (z + 2) % 4
    right, left = (yh * 4 + xp, col), (yh * 4 + xm, col)
    up, down = (row, zp * 4 + col % 4), (row, zm * 4 + col % 4)
    yrow = (1 - yh) * 4 + x
    ycol = z * 4 + (1 - yl) * 2 + core
    opp = (yrow, col)
    mate = (row, z * 4 + yl * 2 + (1 - core))

    def rc(src, dst, k, dev):
        return pltpu.make_async_remote_copy(
            src_ref=src, dst_ref=dst, send_sem=ssem.at[k], recv_sem=rsem.at[k],
            device_id=dev, device_id_type=MESH,
        )

    bar = pltpu.get_barrier_semaphore()

    def greet(d, carry):
        pl.semaphore_signal(bar, inc=1, device_id=(row, col ^ d), device_id_type=MESH)
        return carry

    lax.fori_loop(1, 16, greet, 0)
    for dev in (right, left, up, down, opp, (yrow, ycol)):
        pl.semaphore_signal(bar, inc=1, device_id=dev, device_id_type=MESH)

    load_t = pltpu.make_async_copy(tt_ref, tt, lsem.at[0])
    load_t.start()

    def upright(lanes, count):
        spread = jnp.broadcast_to(lanes, (count, count))
        at = lax.broadcasted_iota(jnp.int32, (count, count), 0) == lax.broadcasted_iota(jnp.int32, (count, count), 1)
        return jnp.sum(jnp.where(at, spread, 0), axis=1, keepdims=True)

    oi_ref[...] = upright(occ_lanes[...], OT)
    vb_ref[...] = upright(virt_lanes[...], VT)
    for a in range(VL):
        ml_ref[:, a * OT : (a + 1) * OT] = occ_lanes[...] ^ virt_ref[row * VL + a]
    for a in range(VC):
        vl_ref[:, a * VT : (a + 1) * VT] = virt_lanes[...] ^ virt_ref[col * VC + a]

    def l_step(a, carry):
        rows = pl.ds(pl.multiple_of(a * VT, VT), VT)
        labels = vb_ref[...] ^ virt_ref[row * VL + a]
        lmask[rows, :] = jnp.where(labels == vl_ref[...], l_ref[rows, :], 0.0)
        return carry

    lax.fori_loop(0, VL, l_step, 0)
    lx[core, z, yme] = lmask[...].T

    for a in range(VL):
        row_e[:, a * VT : (a + 1) * VT] = ve_lanes[...] + ve_ref[row * VL + a]
    for i in range(OL):
        col_e[:, i * OT : (i + 1) * OT] = oe_lanes[...] + oe_ref[col * OL + i]
    load_t.wait()
    for h in range(2):
        high, low = split2(tt[h])
        part_s = dot_nt(p_ref[...], high) + dot_nt(p_ref[...], low)
        for i in range(OL // 2):
            to = (h * 3 + i) * OT
            s_ref[:, to : to + OT] = part_s[:, i * OT : (i + 1) * OT]
    pl.semaphore_wait(bar, 21)

    def peer(ref, index):
        return ref.at[pl.ds(pl.multiple_of(index * 32, 32), 32), :]

    def a2a_copy(d):
        return rc(peer(s_ref, col ^ d), peer(raw, col), A2A + d, (row, col ^ d))

    yt = rc(tt_ref.at[1 - yh], tx.at[x, yh], YT, opp)
    yt.start()
    x1 = [rc(tt_ref.at[yh], tx.at[x, yh], X1 + n, dev) for n, dev in enumerate((right, left))]
    for copy in x1:
        copy.start()
    lax.fori_loop(1, 16, lambda d, n: (a2a_copy(d).start(), n)[1], 0)
    own_t = pltpu.make_async_copy(tt_ref.at[yh], tx.at[x, yh], lsem.at[0])
    own_t.start()
    own_s = pltpu.make_async_copy(peer(s_ref, col), peer(raw, col), lsem.at[1])
    own_s.start()
    own_l = lx.at[core, z, yme]
    ydevs = [(row, ycol), (yrow, ycol), opp]
    yidx = [yh * 2 + 1 - yl, (1 - yh) * 2 + 1 - yl, (1 - yh) * 2 + yl]
    ly = [rc(own_l, own_l, LY + n, dev) for n, dev in enumerate(ydevs)]
    for copy in ly:
        copy.start()
    lz = [rc(own_l, own_l, LZ + n, dev) for n, dev in enumerate((up, down))]
    for copy in lz:
        copy.start()

    order = [(xo, 1 - yh), (xo, yh), (xm, 1 - yh), (xp, 1 - yh), (xp, yh), (xm, yh), (x, 1 - yh), (x, yh)]

    def w_copy(t):
        dx, dy = order[t]
        return pltpu.make_async_copy(w_ref.at[dy * 4 + dx], wbuf.at[t % 2], wsem.at[t % 2])

    w_copy(0).start()
    w_copy(1).start()

    def w_split(t):
        dx, dy = order[t]
        own = ml_ref[...]

        def step(a, carry):
            rows = pl.ds(pl.multiple_of(a * OT, OT), OT)
            labels = oi_ref[...] ^ virt_ref[(dy * 4 + dx) * VL + a]
            kept = jnp.where(labels == own, wbuf[t % 2, rows, :], 0.0)
            high, low = split2(kept)
            w_hi[rows, :] = high
            w_lo[rows, :] = low
            return carry

        lax.fori_loop(0, VL, step, 0)

    def w_mm(t):
        def step(n, carry):
            rows = pl.ds(pl.multiple_of(n * 256, 256), 256)
            high, low = w_hi[rows, :], w_lo[rows, :]
            part[t, rows, :] = dot(high, ca_hi[...]) + dot(high, ca_lo[...]) + dot(low, ca_hi[...])
            return carry

        lax.fori_loop(0, CK // 256, step, 0)

    def cyc(t):
        if t > 0:
            w_copy(t).wait()
            w_split(t)
            if t + 2 < 8:
                w_copy(t + 2).start()
        w_mm(t)

    def add_into(dst, src):
        def step(n, carry):
            rows = pl.ds(pl.multiple_of(n * 96, 96), 96)
            dst[rows, :] = dst[rows, :] + src[rows, :]
            return carry

        lax.fori_loop(0, CK // 96, step, 0)

    w_copy(0).wait()
    w_split(0)
    w_copy(2).start()

    own_t.wait()
    yt.wait_send()
    pltpu.make_async_remote_copy(
        src_ref=tt_ref.at[1 - yh], dst_ref=tx.at[x, 1 - yh], send_sem=ssem.at[YT], recv_sem=rsem.at[YT],
        device_id=opp, device_id_type=MESH,
    ).wait_recv()
    x1b = [rc(tx.at[x, 1 - yh], tx.at[x, 1 - yh], X1 + 2 + n, dev) for n, dev in enumerate((right, left))]
    for copy in x1b:
        copy.start()

    x2 = []

    def pass_on(h, late):
        base = X1 + 2 * late
        rc(tx.at[xm, h], tx.at[xm, h], base, left).wait_recv()
        rc(tx.at[xp, h], tx.at[xp, h], base + 1, right).wait_recv()
        for n, (sx, rows, dev) in enumerate(((xm, upper, right), (xp, lower, left))):
            copy = rc(tx.at[sx, h, rows], tx.at[sx, h, rows], X2 + 2 * late + n, dev)
            copy.start()
            x2.append(copy)

    upper, lower = pl.ds(0, HIJ // 2), pl.ds(HIJ // 2, HIJ // 2)
    pass_on(yh, 0)

    own_s.wait()

    def a2a_wait(d, carry):
        a2a_copy(d).wait_send()
        rc(peer(s_ref, col), peer(raw, col ^ d), A2A + d, (row, col ^ d)).wait_recv()
        return carry

    lax.fori_loop(1, 16, a2a_wait, 0)

    def ca_step(c, carry):
        for i in range(OL):
            parts = [
                raw[pl.ds(pl.multiple_of(c * 32 + b * VL, VL), VL), i * OT : (i + 1) * OT] for b in range(VC)
            ]
            wide = jnp.concatenate(parts, axis=1)
            for n in range(3):
                ca[n, pl.ds(c * OL + i, VL, stride=OT), :] = wide[:, n * THIRD : (n + 1) * THIRD]
        return carry

    lax.fori_loop(0, 16, ca_step, 0)
    for n in range(3):
        high, low = split2(ca[n])
        ca_hi[:, n * THIRD : (n + 1) * THIRD] = high
        ca_lo[:, n * THIRD : (n + 1) * THIRD] = low

    rs = [
        rc(part.at[0], recv.at[0], RS + 0, right),
        rc(part.at[1], recv.at[1], RS + 1, left),
    ]
    lanes3 = [pl.ds(n * THIRD, THIRD) for n in range(3)]
    slot_dev = {2: left, 3: right, 4: right, 5: left}
    rs3 = {
        t: [
            rc(part.at[t, :, lanes], recv.at[t, :, lanes], RS + 2 + (t - 2) * 3 + n, slot_dev[t])
            for n, lanes in enumerate(lanes3)
        ]
        for t in slot_dev
    }

    def send3(t):
        for copy in rs3[t]:
            copy.start()

    cyc(0)
    rs[0].start()
    cyc(1)
    rs[1].start()

    for n, dst_y in enumerate(yidx):
        ly[n].wait_send()
        block = lx.at[core, z, dst_y]
        rc(own_l, block, LY + n, ydevs[n]).wait_recv()
        for m, dev in enumerate((up, down)):
            copy = rc(block, block, LZ + 2 + 2 * n + m, dev)
            copy.start()
            lz.append(copy)
    lc = [rc(lx.at[core, zz], lx.at[core, zz], LC + n, mate) for n, zz in enumerate((z, zm, zp, zo))]
    lc[0].start()

    cyc(2)
    send3(2)
    cyc(3)
    rs[0].wait_recv()
    add_into(part.at[3], recv.at[0])
    send3(3)
    pass_on(1 - yh, 1)
    cyc(4)
    send3(4)
    cyc(5)
    rs[1].wait_recv()
    add_into(part.at[5], recv.at[1])
    send3(5)

    for n, src_y in enumerate([yme] + yidx):
        rc(lx.at[core, zm, src_y], lx.at[core, zm, src_y], LZ + 2 * n, down).wait_recv()
        rc(lx.at[core, zp, src_y], lx.at[core, zp, src_y], LZ + 2 * n + 1, up).wait_recv()
    lz2 = [
        rc(lx.at[core, zm, pl.ds(0, 2)], lx.at[core, zm, pl.ds(0, 2)], LZ2 + 0, up),
        rc(lx.at[core, zp, pl.ds(2, 2)], lx.at[core, zp, pl.ds(2, 2)], LZ2 + 1, down),
    ]
    for copy in lz2:
        copy.start()
    lc[1].start()
    lc[2].start()

    cyc(6)
    cyc(7)

    yr = []
    for n, lanes in enumerate(lanes3):
        rs3[3][n].wait_recv()
        rs3[2][n].wait_recv()
        part[6, :, lanes] = part[6, :, lanes] + (recv[3, :, lanes] + recv[2, :, lanes])
        copy = rc(part.at[6, :, lanes], yrecv.at[:, lanes], YR + n, opp)
        copy.start()
        yr.append(copy)

    rc(lx.at[core, zo, pl.ds(0, 2)], lx.at[core, zo, pl.ds(0, 2)], LZ2 + 0, down).wait_recv()
    rc(lx.at[core, zo, pl.ds(2, 2)], lx.at[core, zo, pl.ds(2, 2)], LZ2 + 1, up).wait_recv()
    lc[3].start()
    for n, zz in enumerate((z, zm, zp, zo)):
        rc(lx.at[1 - core, zz], lx.at[1 - core, zz], LC + n, mate).wait_recv()

    for h in range(2):
        oacc[h] = jnp.zeros((HIJ, AB), F32)

    def ladder(sx, n):
        kc, sy = n // 2, n % 2
        source = sy * 4 + sx
        zz, ylo = source // 2, source % 2
        lanes = pl.ds(pl.multiple_of(kc * CD, CD), CD)
        t_hi, t_lo = split2(tx[sx, sy, :, lanes])
        both = jnp.concatenate([t_hi, t_lo], axis=0)
        for h in range(2):
            high, low = split2(lx[kc, zz, h * 2 + ylo])
            wide = dot(both, high)
            oacc[h] = oacc[h] + (wide[:HIJ] + wide[HIJ:] + dot(t_hi, low))

    def ladder_run(sx):
        lax.fori_loop(0, 4, lambda n, carry: (ladder(sx, n), carry)[1], 0)

    def back_copy(n, d):
        return rc(
            cp.at[col ^ d, :, lanes3[n]], d_ref.at[col, :, lanes3[n]], BACK + 16 * n + d, (row, col ^ d)
        )

    own_d = [
        pltpu.make_async_copy(cp.at[col, :, lanes], d_ref.at[col, :, lanes], lsem.at[1 + n])
        for n, lanes in enumerate(lanes3)
    ]

    def finish(n):
        lanes = lanes3[n]
        rs3[4][n].wait_recv()
        rs3[5][n].wait_recv()
        yr[n].wait_recv()
        value = (part[7, :, lanes] + recv[4, :, lanes]) + (recv[5, :, lanes] + yrecv[:, lanes])
        high, low = split2(value)
        rest = (value - high.astype(F32) - low.astype(F32)).astype(BF16)
        sel = q_ref[...]
        cp[:, :, lanes] = (dot(sel, high) + dot(sel, low) + dot(sel, rest)).reshape(16, BLK, THIRD)
        lax.fori_loop(1, 16, lambda d, carry: (back_copy(n, d).start(), carry)[1], 0)
        own_d[n].start()

    ladder_run(x)
    ladder_run(xm)
    ladder_run(xp)
    finish(0)
    for base, sx, rows, dev in ((0, xo, upper, left), (1, xo, lower, right)):
        for h, late in ((yh, 0), (1 - yh, 1)):
            rc(tx.at[sx, h, rows], tx.at[sx, h, rows], X2 + 2 * late + base, dev).wait_recv()
    ladder_run(xo)
    out_own = pltpu.make_async_copy(oacc.at[yh], lo_ref.at[yh], lsem.at[0])
    out_own.start()
    ob = rc(oacc.at[1 - yh], lo_ref.at[yh], OB, opp)
    ob.start()
    finish(1)
    finish(2)

    for copy in x1 + x1b + x2 + lz + lz2 + lc + rs + sum(rs3.values(), []) + yr + [ob]:
        copy.wait_send()
    rc(oacc.at[yh], lo_ref.at[1 - yh], OB, opp).wait_recv()
    out_own.wait()
    for n, lanes in enumerate(lanes3):
        own_d[n].wait()

        def back_wait(d, carry):
            back_copy(n, d).wait_send()
            rc(
                cp.at[col, :, lanes], d_ref.at[col ^ d, :, lanes], BACK + 16 * n + d, (row, col ^ d)
            ).wait_recv()
            return carry

        lax.fori_loop(1, 16, back_wait, 0)


def to_peers():
    c, b, a = np.meshgrid(np.arange(16), np.arange(VC), np.arange(VL), indexing="ij")
    table = np.zeros((AB, AB), np.float32)
    table[(c * 32 + b * VL + a).reshape(-1), (a * VT + c * VC + b).reshape(-1)] = 1.0
    return table


def from_cycle():
    a, c, i = np.meshgrid(np.arange(VL), np.arange(16), np.arange(OL), indexing="ij")
    table = np.zeros((CK, CK), np.float32)
    table[(c * BLK + a * OL + i).reshape(-1), (a * OT + c * OL + i).reshape(-1)] = 1.0
    return table


def body(amps, ladder_ints, cycle_ints, virt_irrep, occ_irrep, virt_energy, occ_energy):
    turned = amps.T.reshape(2, HIJ, AB)
    anywhere = pl.BlockSpec(memory_space=pl.ANY)
    vmem = pl.BlockSpec(memory_space=pltpu.VMEM)
    smem = pl.BlockSpec(memory_space=pltpu.SMEM)
    ladder, cycle, row_energy, col_energy = pl.pallas_call(
        kernel,
        out_shape=(
            jax.ShapeDtypeStruct((2, HIJ, AB), F32),
            jax.ShapeDtypeStruct((16, BLK, BJ), F32),
            jax.ShapeDtypeStruct((1, AB), F32),
            jax.ShapeDtypeStruct((1, OL * OT), F32),
        ),
        in_specs=[smem] * 3 + [anywhere, vmem, anywhere] + [vmem] * 6,
        out_specs=(anywhere, anywhere, vmem, vmem),
        scratch_shapes=[
            pltpu.VMEM((2, HIJ, AB), F32),
            pltpu.VMEM((AB, OL * OT), F32),
            pltpu.VMEM((4, 2, HIJ, AB), F32),
            pltpu.VMEM((2, 4, 4, CD, AB), F32),
            pltpu.VMEM((AB, OL * OT), F32),
            pltpu.VMEM((3, CK, THIRD), F32),
            pltpu.VMEM((CK, BJ), BF16),
            pltpu.VMEM((CK, BJ), BF16),
            pltpu.VMEM((2, CK, CK), F32),
            pltpu.VMEM((CK, CK), BF16),
            pltpu.VMEM((CK, CK), BF16),
            pltpu.VMEM((8, CK, BJ), F32),
            pltpu.VMEM((6, CK, BJ), F32),
            pltpu.VMEM((CK, BJ), F32),
            pltpu.VMEM((2, HIJ, AB), F32),
            pltpu.VMEM((AB, CD), F32),
            pltpu.VMEM((16, BLK, BJ), F32),
            pltpu.VMEM((1, CK), jnp.int32),
            pltpu.VMEM((1, CD), jnp.int32),
            pltpu.VMEM((OT, 1), jnp.int32),
            pltpu.VMEM((VT, 1), jnp.int32),
            pltpu.SemaphoreType.DMA((NSEM,)),
            pltpu.SemaphoreType.DMA((NSEM,)),
            pltpu.SemaphoreType.DMA((2,)),
            pltpu.SemaphoreType.DMA((4,)),
        ],
        compiler_params=pltpu.CompilerParams(
            collective_id=0, has_side_effects=True, vmem_limit_bytes=67043328
        ),
    )(
        virt_irrep, virt_energy, occ_energy, turned, ladder_ints, cycle_ints.reshape(8, CK, CK),
        virt_irrep.reshape(1, VT), occ_irrep.reshape(1, OT), virt_energy.reshape(1, VT), occ_energy.reshape(1, OT),
        jnp.asarray(to_peers(), BF16), jnp.asarray(from_cycle(), BF16),
    )
    back = cycle.reshape(16, VL, OL, VC, OT).transpose(2, 4, 1, 0, 3).reshape(OL * OT, AB)
    return ((ladder.reshape(OL * OT, AB) + back) / (row_energy - col_energy.reshape(OL * OT, 1))).T


def solution(mesh):
    placed = (P("row", "col"), P("row", "col"), P(None, "row"), P(), P(), P(), P())
    return jax.shard_map(
        body, mesh=mesh, in_specs=placed, out_specs=P("row", "col"), check_vma=False
    )
```

time: 177 us -> 160 us (0.904)
  local copies, waits for them, and re-layouts: 19.5 us -> 9.75 us
  Pallas kernels: 154 us -> 149 us
    pallas_call x1, Pallas kernels: 154 us -> 149 us  [body(): pl.pallas_call(kernel, out_shape=(jax.ShapeDtypeStruct((2, HIJ, AB), F32)...]
    reshape x5 -> x3, local copies, waits for them, and re-layouts: 9.09 us -> 5.35 us  [body(): cycle.reshape(16, VL, OL, VC, OT).transpose(2, 4, 1, 0, 3)]
    transpose x2 -> x1, local copies, waits for them, and re-layouts: 4.29 us -> 2.71 us  [body(): return ((ladder.reshape(OL * OT, AB) + back) / (row_energy - col_energy.r...]
where the time goes in v3:
time: 160 us
  Pallas kernels  149 us (93%)
  local copies, waits for them, and re-layouts  9.75 us (6%)
    pallas_call x1, Pallas kernels, body(): pl.pallas_call(kernel, out_shape=(jax.ShapeDtypeStruct((2, HIJ, AB), F32)...  149 us
    reshape x3, local copies, waits for them, and re-layouts, body(): cycle.reshape(16, VL, OL, VC, OT).transpose(2, 4, 1, 0, 3)  5.35 us

profile of v3, /device:TPU:0, one launch (start us, length us, event | category | flops | bytes accessed | tf_op | source)
XLA Modules:
  0.0 159.7 jit_solution(17067026962387527029)
XLA Ops:
  0.0 148.5 %shard_map.91 = (f32[2,288,512]{2,1,0:T(8,128)}, f32[16,48,384]{2,1,0:T(8,128)}, f32[1,512]{1,0:T(1,128)}, f32[1,576]{1,0:T(1,128)}) custom-call(s32[64]{0:T(128)} %virt_ref.1, f32[64]{0:T(128)} %ve_ref.1, f32[96]{0:T(128)} %oe_ref.1, f32[2,288,512]{2,1,0:T(8,128)} %bitcast.20, f32[512,256]{1,0:T(8,128)} %l_ref.1, f32[8,768,768]{2,1,0:T(8,128)} %bitcast.17, ...), custom_call_target="tpu_custom_call" | custom-call | tf_op jit(solution)/shard_map/pallas_call | solution.py:413
  148.5 3.1 %reshape.36 = f32[16,8,6,4,96]{4,3,2,1,0:T(4,128)} reshape(f32[16,48,384]{2,1,0:T(8,128)} %get-tuple-element.10) | data formatting | bytes 2359296 | tf_op jit(solution)/shard_map/reshape | solution.py:458
  151.6 1.7 %copy.15 = f32[16,8,6,4,96]{4,2,3,0,1:T(8,128)S(1)} copy(f32[16,8,6,4,96]{4,3,2,1,0:T(4,128)} %reshape.36) | data formatting | bytes 2359296 | tf_op jit(solution)/shard_map/reshape | solution.py:458
  153.4 0.5 reshape.37
  153.9 0.0 copy-start
  153.9 0.0 copy-start.1
  153.9 1.7 %copy.12 = f32[576,512]{0,1:T(8,128)S(1)} copy(f32[576,512]{1,0:T(8,128)} %bitcast.19) | data formatting | bytes 2359296 | tf_op jit(solution)/shard_map/reshape | solution.py:459
  155.6 0.0 copy-done
  155.6 0.0 copy-done.1
  155.6 1.3 divide_bitcast_fusion
  157.0 2.7 %copy.13 = f32[512,576]{0,1:T(8,128)} copy(f32[512,576]{1,0:T(8,128)} %divide_bitcast_fusion) | data formatting | bytes 2359296 | tf_op jit(solution)/shard_map/transpose | solution.py:459
  (1 shorter events, 0.0 us)
Async XLA Ops:
  153.9 1.7 %copy-start = (f32[1,576]{1,0:T(1,128)S(1)}, f32[1,576]{1,0:T(1,128)}, u32[]{:S(2)}) copy-start(f32[1,576]{1,0:T(1,128)} %get-tuple-element.12) | copy-start | bytes 6916
  153.9 1.7 %copy-start.1 = (f32[1,512]{1,0:T(1,128)S(1)}, f32[1,512]{1,0:T(1,128)}, u32[]{:S(2)}) copy-start(f32[1,512]{1,0:T(1,128)} %get-tuple-element.11) | copy-start | bytes 6148

commit v4 on v3

--- a/solution.py
+++ b/solution.py
@@ -22,8 +22,8 @@
 HIJ = OL * OT // 2
 
 A2A, BACK, YT, X1, X2, LY = 0, 16, 64, 65, 69, 73
-LZ, LZ2, LC, OB, RS, YR = 76, 84, 86, 90, 91, 105
-NSEM = 108
+LZ, LZ2, LC, OB, RS, YR, LY2 = 76, 84, 92, 96, 97, 114, 117
+NSEM = 119
 
 
 def split2(value):
@@ -42,8 +42,8 @@
 
 def kernel(
     virt_ref, ve_ref, oe_ref, tt_ref, l_ref, w_ref, virt_lanes, occ_lanes, ve_lanes, oe_lanes, p_ref, q_ref,
-    lo_ref, d_ref, row_e, col_e,
-    tt, s_ref, tx, lx, raw, ca, ca_hi, ca_lo, wbuf, w_hi, w_lo, part, recv, yrecv, oacc, lmask, cp, ml_ref, vl_ref, oi_ref, vb_ref,
+    out_ref,
+    row_s, oe_up, lad, tt, s_ref, tx, lx, raw, ca, ca_hi, ca_lo, wbuf, w_hi, w_lo, part, recv, yrecv, oacc, lmask, cp, d3, ml_ref, vl_ref, oi_ref, vb_ref,
     ssem, rsem, wsem, lsem,
 ):
     row, col = lax.axis_index("row"), lax.axis_index("col")
@@ -81,7 +81,7 @@
     def upright(lanes, count):
         spread = jnp.broadcast_to(lanes, (count, count))
         at = lax.broadcasted_iota(jnp.int32, (count, count), 0) == lax.broadcasted_iota(jnp.int32, (count, count), 1)
-        return jnp.sum(jnp.where(at, spread, 0), axis=1, keepdims=True)
+        return jnp.sum(jnp.where(at, spread, jnp.zeros_like(spread)), axis=1, keepdims=True)
 
     oi_ref[...] = upright(occ_lanes[...], OT)
     vb_ref[...] = upright(virt_lanes[...], VT)
@@ -100,9 +100,8 @@
     lx[core, z, yme] = lmask[...].T
 
     for a in range(VL):
-        row_e[:, a * VT : (a + 1) * VT] = ve_lanes[...] + ve_ref[row * VL + a]
-    for i in range(OL):
-        col_e[:, i * OT : (i + 1) * OT] = oe_lanes[...] + oe_ref[col * OL + i]
+        row_s[:, a * VT : (a + 1) * VT] = ve_lanes[...] + ve_ref[row * VL + a]
+    oe_up[...] = upright(oe_lanes[...], OT)
     load_t.wait()
     for h in range(2):
         high, low = split2(tt[h])
@@ -131,14 +130,14 @@
     own_l = lx.at[core, z, yme]
     ydevs = [(row, ycol), (yrow, ycol), opp]
     yidx = [yh * 2 + 1 - yl, (1 - yh) * 2 + 1 - yl, (1 - yh) * 2 + yl]
-    ly = [rc(own_l, own_l, LY + n, dev) for n, dev in enumerate(ydevs)]
-    for copy in ly:
-        copy.start()
+    ly = [rc(own_l, own_l, LY + n, dev) for n, dev in enumerate(ydevs[:2])]
+    ly[0].start()
+    ly[1].start()
     lz = [rc(own_l, own_l, LZ + n, dev) for n, dev in enumerate((up, down))]
     for copy in lz:
         copy.start()
 
-    order = [(xo, 1 - yh), (xo, yh), (xm, 1 - yh), (xp, 1 - yh), (xp, yh), (xm, yh), (x, 1 - yh), (x, yh)]
+    order = [(xp, 1 - yh), (xm, 1 - yh), (xo, 1 - yh), (xo, yh), (xp, yh), (xm, yh), (x, 1 - yh), (x, yh)]
 
     def w_copy(t):
         dx, dy = order[t]
@@ -215,6 +214,19 @@
     upper, lower = pl.ds(0, HIJ // 2), pl.ds(HIJ // 2, HIJ // 2)
     pass_on(yh, 0)
 
+    lz2 = []
+
+    def pass_block(n, src_y):
+        rc(lx.at[core, zm, src_y], lx.at[core, zm, src_y], LZ + 2 * n, down).wait_recv()
+        rc(lx.at[core, zp, src_y], lx.at[core, zp, src_y], LZ + 2 * n + 1, up).wait_recv()
+        for m, (sz, first, dev) in enumerate(((zm, 0, up), (zp, CD // 2, down))):
+            piece = lx.at[core, sz, src_y, pl.ds(first, CD // 2)]
+            copy = rc(piece, piece, LZ2 + 2 * n + m, dev)
+            copy.start()
+            lz2.append(copy)
+
+    pass_block(0, yme)
+
     own_s.wait()
 
     def a2a_wait(d, carry):
@@ -240,89 +252,111 @@
         ca_hi[:, n * THIRD : (n + 1) * THIRD] = high
         ca_lo[:, n * THIRD : (n + 1) * THIRD] = low
 
-    rs = [
+    lanes3 = [pl.ds(n * THIRD, THIRD) for n in range(3)]
+    top, bottom = pl.ds(0, CK // 2), pl.ds(CK // 2, CK // 2)
+    direct = [
         rc(part.at[0], recv.at[0], RS + 0, right),
         rc(part.at[1], recv.at[1], RS + 1, left),
+        rc(part.at[2], recv.at[2], RS + 2, opp),
+        rc(part.at[4, bottom], recv.at[4, bottom], RS + 3, right),
+        rc(part.at[5, top], recv.at[5, top], RS + 4, left),
     ]
-    lanes3 = [pl.ds(n * THIRD, THIRD) for n in range(3)]
-    slot_dev = {2: left, 3: right, 4: right, 5: left}
-    rs3 = {
-        t: [
-            rc(part.at[t, :, lanes], recv.at[t, :, lanes], RS + 2 + (t - 2) * 3 + n, slot_dev[t])
-            for n, lanes in enumerate(lanes3)
+    first_hop = [
+        [
+            rc(part.at[3, rows, lanes], recv.at[3, rows, lanes], RS + 5 + 3 * m + n, dev)
+            for m, (rows, dev) in enumerate(((top, right), (bottom, left)))
         ]
-        for t in slot_dev
-    }
-
-    def send3(t):
-        for copy in rs3[t]:
+        for n, lanes in enumerate(lanes3)
+    ]
+    second_hop = [
+        [
+            rc(part.at[t, rows, lanes], recv.at[t, rows, lanes], RS + 11 + 3 * m + n, dev)
+            for m, (t, rows, dev) in enumerate(((4, top, right), (5, bottom, left)))
+        ]
+        for n, lanes in enumerate(lanes3)
+    ]
+    mine, other = [pl.ds(pl.multiple_of(h * (CD // 2), CD // 2), CD // 2) for h in (yh, 1 - yh)]
+
+    def over_z(n):
+        block = lx.at[core, z, yidx[n]]
+        if n < 2:
+            rc(own_l, block, LY + n, ydevs[n]).wait_recv()
+            piece = lx.at[core, z, yidx[n], mine]
+            copy = rc(piece, piece, LY2 + n, ydevs[1 - n])
             copy.start()
-
-    cyc(0)
-    rs[0].start()
-    cyc(1)
-    rs[1].start()
-
-    for n, dst_y in enumerate(yidx):
-        ly[n].wait_send()
-        block = lx.at[core, z, dst_y]
-        rc(own_l, block, LY + n, ydevs[n]).wait_recv()
+            ly.append(copy)
+        else:
+            for m, rows in ((0, other), (1, mine)):
+                piece = lx.at[core, z, yidx[n], rows]
+                rc(piece, piece, LY2 + m, ydevs[1 - m]).wait_recv()
         for m, dev in enumerate((up, down)):
             copy = rc(block, block, LZ + 2 + 2 * n + m, dev)
             copy.start()
             lz.append(copy)
+
+    cyc(0)
+    direct[0].start()
+    pass_on(1 - yh, 1)
+    over_z(0)
+    over_z(1)
+    cyc(1)
+    direct[1].start()
+    cyc(2)
+    direct[2].start()
+
+    over_z(2)
     lc = [rc(lx.at[core, zz], lx.at[core, zz], LC + n, mate) for n, zz in enumerate((z, zm, zp, zo))]
     lc[0].start()
 
-    cyc(2)
-    send3(2)
     cyc(3)
-    rs[0].wait_recv()
-    add_into(part.at[3], recv.at[0])
-    send3(3)
-    pass_on(1 - yh, 1)
     cyc(4)
-    send3(4)
+    direct[3].start()
     cyc(5)
-    rs[1].wait_recv()
-    add_into(part.at[5], recv.at[1])
-    send3(5)
-
-    for n, src_y in enumerate([yme] + yidx):
-        rc(lx.at[core, zm, src_y], lx.at[core, zm, src_y], LZ + 2 * n, down).wait_recv()
-        rc(lx.at[core, zp, src_y], lx.at[core, zp, src_y], LZ + 2 * n + 1, up).wait_recv()
-    lz2 = [
-        rc(lx.at[core, zm, pl.ds(0, 2)], lx.at[core, zm, pl.ds(0, 2)], LZ2 + 0, up),
-        rc(lx.at[core, zp, pl.ds(2, 2)], lx.at[core, zp, pl.ds(2, 2)], LZ2 + 1, down),
-    ]
-    for copy in lz2:
-        copy.start()
-    lc[1].start()
-    lc[2].start()
-
+    direct[4].start()
+    pass_block(1, yidx[0])
+    pass_block(2, yidx[1])
     cyc(6)
     cyc(7)
 
+    direct[0].wait_recv()
+    direct[1].wait_recv()
     yr = []
     for n, lanes in enumerate(lanes3):
-        rs3[3][n].wait_recv()
-        rs3[2][n].wait_recv()
-        part[6, :, lanes] = part[6, :, lanes] + (recv[3, :, lanes] + recv[2, :, lanes])
+        part[6, :, lanes] = part[6, :, lanes] + (recv[0, :, lanes] + recv[1, :, lanes])
         copy = rc(part.at[6, :, lanes], yrecv.at[:, lanes], YR + n, opp)
         copy.start()
         yr.append(copy)
 
-    rc(lx.at[core, zo, pl.ds(0, 2)], lx.at[core, zo, pl.ds(0, 2)], LZ2 + 0, down).wait_recv()
-    rc(lx.at[core, zo, pl.ds(2, 2)], lx.at[core, zo, pl.ds(2, 2)], LZ2 + 1, up).wait_recv()
+    pass_block(3, yidx[2])
+    lc[1].start()
+    lc[2].start()
+
+    direct[2].wait_recv()
+    for n, lanes in enumerate(lanes3):
+        part[3, :, lanes] = part[3, :, lanes] + recv[2, :, lanes]
+        for copy in first_hop[n]:
+            copy.start()
+
+    def relay(n):
+        lanes = lanes3[n]
+        for m, (t, rows) in enumerate(((4, top), (5, bottom))):
+            first_hop[n][m].wait_recv()
+            part[t, rows, lanes] = part[t, rows, lanes] + recv[3, rows, lanes]
+            second_hop[n][m].start()
+
+    relay(0)
+    relay(1)
+
+    for n, src_y in enumerate([yme] + yidx):
+        for m, (first, dev) in enumerate(((0, down), (CD // 2, up))):
+            piece = lx.at[core, zo, src_y, pl.ds(first, CD // 2)]
+            rc(piece, piece, LZ2 + 2 * n + m, dev).wait_recv()
     lc[3].start()
-    for n, zz in enumerate((z, zm, zp, zo)):
-        rc(lx.at[1 - core, zz], lx.at[1 - core, zz], LC + n, mate).wait_recv()
 
     for h in range(2):
         oacc[h] = jnp.zeros((HIJ, AB), F32)
 
-    def ladder(sx, n):
-        kc, sy = n // 2, n % 2
+    def ladder(sx, kc, sy):
         source = sy * 4 + sx
         zz, ylo = source // 2, source % 2
         lanes = pl.ds(pl.multiple_of(kc * CD, CD), CD)
@@ -333,62 +367,89 @@
             wide = dot(both, high)
             oacc[h] = oacc[h] + (wide[:HIJ] + wide[HIJ:] + dot(t_hi, low))
 
-    def ladder_run(sx):
-        lax.fori_loop(0, 4, lambda n, carry: (ladder(sx, n), carry)[1], 0)
+    def ladder_run(kc):
+        lax.fori_loop(0, 8, lambda n, carry: (ladder(n % 4, kc, n // 4), carry)[1], 0)
 
     def back_copy(n, d):
         return rc(
-            cp.at[col ^ d, :, lanes3[n]], d_ref.at[col, :, lanes3[n]], BACK + 16 * n + d, (row, col ^ d)
+            cp.at[n, col ^ d], d3.at[n, col], BACK + 16 * n + d, (row, col ^ d)
         )
 
     own_d = [
-        pltpu.make_async_copy(cp.at[col, :, lanes], d_ref.at[col, :, lanes], lsem.at[1 + n])
+        pltpu.make_async_copy(cp.at[n, col], d3.at[n, col], lsem.at[1 + n])
         for n, lanes in enumerate(lanes3)
     ]
 
     def finish(n):
         lanes = lanes3[n]
-        rs3[4][n].wait_recv()
-        rs3[5][n].wait_recv()
-        yr[n].wait_recv()
+        for copy in second_hop[n] + [yr[n]]:
+            copy.wait_recv()
+        if n == 0:
+            direct[3].wait_recv()
+            direct[4].wait_recv()
         value = (part[7, :, lanes] + recv[4, :, lanes]) + (recv[5, :, lanes] + yrecv[:, lanes])
         high, low = split2(value)
         rest = (value - high.astype(F32) - low.astype(F32)).astype(BF16)
         sel = q_ref[...]
-        cp[:, :, lanes] = (dot(sel, high) + dot(sel, low) + dot(sel, rest)).reshape(16, BLK, THIRD)
+        cp[n] = (dot(sel, high) + dot(sel, low) + dot(sel, rest)).reshape(16, BLK, THIRD)
         lax.fori_loop(1, 16, lambda d, carry: (back_copy(n, d).start(), carry)[1], 0)
         own_d[n].start()
 
-    ladder_run(x)
-    ladder_run(xm)
-    ladder_run(xp)
+    for base, rows, dev in ((0, upper, left), (1, lower, right)):
+        for h, late in ((yh, 0), (1 - yh, 1)):
+            rc(tx.at[xo, h, rows], tx.at[xo, h, rows], X2 + 2 * late + base, dev).wait_recv()
+    ladder_run(core)
+    relay(2)
     finish(0)
-    for base, sx, rows, dev in ((0, xo, upper, left), (1, xo, lower, right)):
-        for h, late in ((yh, 0), (1 - yh, 1)):
-            rc(tx.at[sx, h, rows], tx.at[sx, h, rows], X2 + 2 * late + base, dev).wait_recv()
-    ladder_run(xo)
-    out_own = pltpu.make_async_copy(oacc.at[yh], lo_ref.at[yh], lsem.at[0])
+    for n, zz in enumerate((z, zm, zp, zo)):
+        rc(lx.at[1 - core, zz], lx.at[1 - core, zz], LC + n, mate).wait_recv()
+    ladder_run(1 - core)
+    out_own = pltpu.make_async_copy(oacc.at[yh], lad.at[yh], lsem.at[0])
     out_own.start()
-    ob = rc(oacc.at[1 - yh], lo_ref.at[yh], OB, opp)
+    ob = rc(oacc.at[1 - yh], lad.at[yh], OB, opp)
     ob.start()
     finish(1)
     finish(2)
 
-    for copy in x1 + x1b + x2 + lz + lz2 + lc + rs + sum(rs3.values(), []) + yr + [ob]:
+    for copy in x1 + x1b + x2 + ly + lz + lz2 + lc + direct + sum(first_hop + second_hop, []) + yr + [ob]:
         copy.wait_send()
-    rc(oacc.at[yh], lo_ref.at[1 - yh], OB, opp).wait_recv()
+    rc(oacc.at[yh], lad.at[1 - yh], OB, opp).wait_recv()
     out_own.wait()
-    for n, lanes in enumerate(lanes3):
+    def unpack(c):
+        wide = [
+            jnp.concatenate([d3[n, c, pl.ds(i, VL, stride=OL), :] for n in range(3)], axis=1) for i in range(OL)
+        ]
+        for b in range(VC):
+            rows = pl.ds(pl.multiple_of(c * 32 + b * VL, VL), VL)
+            raw[rows, :] = jnp.concatenate([value[:, b * OT : (b + 1) * OT] for value in wide], axis=1)
+
+    for n in range(3):
         own_d[n].wait()
 
         def back_wait(d, carry):
-            back_copy(n, d).wait_send()
-            rc(
-                cp.at[col, :, lanes], d_ref.at[col ^ d, :, lanes], BACK + 16 * n + d, (row, col ^ d)
-            ).wait_recv()
+            leaving = back_copy(n, d)
+            leaving.wait_send()
+            arriving = rc(cp.at[n, col], d3.at[n, col ^ d], BACK + 16 * n + d, (row, col ^ d))
+            arriving.wait_recv()
+            if n == 2:
+                unpack(col ^ d)
             return carry
 
+        if n == 2:
+            unpack(col)
         lax.fori_loop(1, 16, back_wait, 0)
+
+    turned = raw[...].T
+    tt[0] = turned[:HIJ]
+    tt[1] = turned[HIJ:]
+    for i in range(OL):
+        h, rows = i // 3, pl.ds((i % 3) * OT, OT)
+        value = tt[h, rows, :]
+        high, low = split2(value)
+        rest = (value - high.astype(F32) - low.astype(F32)).astype(BF16)
+        sel = p_ref[...]
+        total = lad[h, rows, :] + (dot(high, sel) + dot(low, sel) + dot(rest, sel))
+        out_ref[i * OT : (i + 1) * OT, :] = total / (row_s[...] - (oe_up[...] + oe_ref[col * OL + i]))
 
 
 def to_peers():
@@ -410,17 +471,15 @@
     anywhere = pl.BlockSpec(memory_space=pl.ANY)
     vmem = pl.BlockSpec(memory_space=pltpu.VMEM)
     smem = pl.BlockSpec(memory_space=pltpu.SMEM)
-    ladder, cycle, row_energy, col_energy = pl.pallas_call(
+    update = pl.pallas_call(
         kernel,
-        out_shape=(
-            jax.ShapeDtypeStruct((2, HIJ, AB), F32),
-            jax.ShapeDtypeStruct((16, BLK, BJ), F32),
-            jax.ShapeDtypeStruct((1, AB), F32),
-            jax.ShapeDtypeStruct((1, OL * OT), F32),
-        ),
+        out_shape=jax.ShapeDtypeStruct((OL * OT, AB), F32),
         in_specs=[smem] * 3 + [anywhere, vmem, anywhere] + [vmem] * 6,
-        out_specs=(anywhere, anywhere, vmem, vmem),
+        out_specs=vmem,
         scratch_shapes=[
+            pltpu.VMEM((1, AB), F32),
+            pltpu.VMEM((OT, 1), F32),
+            pltpu.VMEM((2, HIJ, AB), F32),
             pltpu.VMEM((2, HIJ, AB), F32),
             pltpu.VMEM((AB, OL * OT), F32),
             pltpu.VMEM((4, 2, HIJ, AB), F32),
@@ -437,7 +496,8 @@
             pltpu.VMEM((CK, BJ), F32),
             pltpu.VMEM((2, HIJ, AB), F32),
             pltpu.VMEM((AB, CD), F32),
-            pltpu.VMEM((16, BLK, BJ), F32),
+            pltpu.VMEM((3, 16, BLK, THIRD), F32),
+            pltpu.VMEM((3, 16, BLK, THIRD), F32),
             pltpu.VMEM((1, CK), jnp.int32),
             pltpu.VMEM((1, CD), jnp.int32),
             pltpu.VMEM((OT, 1), jnp.int32),
@@ -445,7 +505,7 @@
             pltpu.SemaphoreType.DMA((NSEM,)),
             pltpu.SemaphoreType.DMA((NSEM,)),
             pltpu.SemaphoreType.DMA((2,)),
-            pltpu.SemaphoreType.DMA((4,)),
+            pltpu.SemaphoreType.DMA((6,)),
         ],
         compiler_params=pltpu.CompilerParams(
             collective_id=0, has_side_effects=True, vmem_limit_bytes=67043328
@@ -455,8 +515,7 @@
         virt_irrep.reshape(1, VT), occ_irrep.reshape(1, OT), virt_energy.reshape(1, VT), occ_energy.reshape(1, OT),
         jnp.asarray(to_peers(), BF16), jnp.asarray(from_cycle(), BF16),
     )
-    back = cycle.reshape(16, VL, OL, VC, OT).transpose(2, 4, 1, 0, 3).reshape(OL * OT, AB)
-    return ((ladder.reshape(OL * OT, AB) + back) / (row_energy - col_energy.reshape(OL * OT, 1))).T
+    return update.T
 
 
 def solution(mesh):

time: 160 us -> 147 us (0.919)
  local copies, waits for them, and re-layouts: 9.75 us -> 2.36 us
  Pallas kernels: 149 us -> 143 us
    reshape x4 -> x0, local copies, waits for them, and re-layouts: 7.02 us -> none  [the longest x3 5.35 us: body(): cycle.reshape(16, VL, OL, VC, OT).transpose(2, 4, 1, 0, 3)]
    pallas_call x1, Pallas kernels: 149 us -> 143 us  [body(): pl.pallas_call(kernel, out_shape=jax.ShapeDtypeStruct((OL * OT, AB), F32)...]
    transpose x1 -> x0, local copies, waits for them, and re-layouts: 2.71 us -> none  [body(): return ((ladder.reshape(OL * OT, AB) + back) / (row_energy - col_energy.r...]
    unnamed x4 -> x1, local copies, waits for them, and re-layouts: 0.01 us -> 2.36 us
where the time goes in v4:
time: 147 us; the launch traced here: 146 us
  Pallas kernels  143 us (97%)
  local copies, waits for them, and re-layouts  2.36 us (2%)
    pallas_call x1, Pallas kernels, body(): pl.pallas_call(kernel, out_shape=jax.ShapeDtypeStruct((OL * OT, AB), F32)...  143 us

profile of v4, /device:TPU:0, one launch (start us, length us, event | category | flops | bytes accessed | tf_op | source)
XLA Modules:
  0.0 145.6 jit_solution(12309969379852664740)
XLA Ops:
  0.0 143.2 %shard_map.91 = f32[576,512]{1,0:T(8,128)} custom-call(s32[64]{0:T(128)} %virt_ref.1, f32[64]{0:T(128)} %ve_ref.1, f32[96]{0:T(128)} %oe_ref.1, f32[2,288,512]{2,1,0:T(8,128)} %bitcast.11, f32[512,256]{1,0:T(8,128)} %l_ref.1, f32[8,768,768]{2,1,0:T(8,128)} %bitcast.9, s32[1,64]{1,0:T(1,128)} %bitcast.12, s32[1,96]{1,0:T(1,128)} %bitcast.15, ...), custom_call_target="tpu_custom_call" | custom-call | tf_op jit(solution)/shard_map/pallas_call | solution.py:474
  143.2 2.4 %copy.11 = f32[512,576]{0,1:T(8,128)} copy(f32[512,576]{0,1:T(8,128)} %bitcast.10) | data formatting | bytes 2359296

commit v5 on v4

--- a/solution.py
+++ b/solution.py
@@ -43,8 +43,8 @@
 def kernel(
     virt_ref, ve_ref, oe_ref, tt_ref, l_ref, w_ref, virt_lanes, occ_lanes, ve_lanes, oe_lanes, p_ref, q_ref,
     out_ref,
-    row_s, oe_up, lad, tt, s_ref, tx, lx, raw, ca, ca_hi, ca_lo, wbuf, w_hi, w_lo, part, recv, yrecv, oacc, lmask, cp, d3, ml_ref, vl_ref, oi_ref, vb_ref,
-    ssem, rsem, wsem, lsem,
+    row_s, oe_up, lad, turned, tt, s_ref, tx, lx, raw, ca, ca_hi, ca_lo, wbuf, w_hi, w_lo, part, recv, yrecv, oacc, lmask, cp, d3, ml_ref, vl_ref, oi_ref, vb_ref,
+    ssem, rsem, wsem, lsem, osem,
 ):
     row, col = lax.axis_index("row"), lax.axis_index("col")
     yh, x = row // 4, row % 4
@@ -398,23 +398,26 @@
     for base, rows, dev in ((0, upper, left), (1, lower, right)):
         for h, late in ((yh, 0), (1 - yh, 1)):
             rc(tx.at[xo, h, rows], tx.at[xo, h, rows], X2 + 2 * late + base, dev).wait_recv()
+    relay(2)
     ladder_run(core)
-    relay(2)
     finish(0)
+    finish(1)
+    finish(2)
     for n, zz in enumerate((z, zm, zp, zo)):
         rc(lx.at[1 - core, zz], lx.at[1 - core, zz], LC + n, mate).wait_recv()
     ladder_run(1 - core)
-    out_own = pltpu.make_async_copy(oacc.at[yh], lad.at[yh], lsem.at[0])
-    out_own.start()
-    ob = rc(oacc.at[1 - yh], lad.at[yh], OB, opp)
-    ob.start()
-    finish(1)
-    finish(2)
-
-    for copy in x1 + x1b + x2 + ly + lz + lz2 + lc + direct + sum(first_hop + second_hop, []) + yr + [ob]:
-        copy.wait_send()
-    rc(oacc.at[yh], lad.at[1 - yh], OB, opp).wait_recv()
-    out_own.wait()
+    bands = [pl.ds(n * OT, OT) for n in range(OL // 2)]
+    ob = [
+        rc(oacc.at[1 - yh, rows], lad.at[yh, rows], k, opp) for rows, k in zip(bands, (OB, LY + 2, BACK))
+    ]
+    for copy in ob:
+        copy.start()
+
+    inverse = tx.at[xo]
+    for h in range(2):
+        for n, rows in enumerate(bands):
+            inverse[h, rows, :] = 1.0 / (row_s[...] - (oe_up[...] + oe_ref[col * OL + h * 3 + n]))
+
     def unpack(c):
         wide = [
             jnp.concatenate([d3[n, c, pl.ds(i, VL, stride=OL), :] for n in range(3)], axis=1) for i in range(OL)
@@ -423,33 +426,62 @@
             rows = pl.ds(pl.multiple_of(c * 32 + b * VL, VL), VL)
             raw[rows, :] = jnp.concatenate([value[:, b * OT : (b + 1) * OT] for value in wide], axis=1)
 
-    for n in range(3):
-        own_d[n].wait()
-
-        def back_wait(d, carry):
+    def back_wait(d):
+        for n in range(3):
             leaving = back_copy(n, d)
             leaving.wait_send()
             arriving = rc(cp.at[n, col], d3.at[n, col ^ d], BACK + 16 * n + d, (row, col ^ d))
             arriving.wait_recv()
-            if n == 2:
-                unpack(col ^ d)
-            return carry
-
-        if n == 2:
-            unpack(col)
-        lax.fori_loop(1, 16, back_wait, 0)
-
-    turned = raw[...].T
-    tt[0] = turned[:HIJ]
-    tt[1] = turned[HIJ:]
+        unpack(col ^ d)
+
+    def gather_rows(ref, group):
+        starts = [pl.multiple_of(zz * 128 + group * 64, 64) for zz in range(4)]
+        return jnp.concatenate([ref[pl.ds(start, 64), :] for start in starts], axis=0)
+
+    def turn(group):
+        xt = gather_rows(raw, group).T
+        turned[0] = xt[:HIJ]
+        turned[1] = xt[HIJ:]
+        return gather_rows(p_ref, group)
+
+    def selected(value, sel):
+        high, low = split2(value)
+        rest = (value - high.astype(F32) - low.astype(F32)).astype(BF16)
+        return dot(high, sel) + dot(low, sel) + dot(rest, sel)
+
+    for n in range(3):
+        own_d[n].wait()
+    unpack(col)
+    lax.fori_loop(1, 8, lambda k, carry: (back_wait((k // 2) * 4 + k % 2), carry)[1], 0)
+    sel = turn(yl)
     for i in range(OL):
         h, rows = i // 3, pl.ds((i % 3) * OT, OT)
-        value = tt[h, rows, :]
-        high, low = split2(value)
-        rest = (value - high.astype(F32) - low.astype(F32)).astype(BF16)
-        sel = p_ref[...]
-        total = lad[h, rows, :] + (dot(high, sel) + dot(low, sel) + dot(rest, sel))
-        out_ref[i * OT : (i + 1) * OT, :] = total / (row_s[...] - (oe_up[...] + oe_ref[col * OL + i]))
+        tt[h, rows, :] = selected(turned[h, rows, :], sel)
+    lax.fori_loop(0, 8, lambda k, carry: (back_wait((k // 2) * 4 + 2 + k % 2), carry)[1], 0)
+    sel = turn(1 - yl)
+    for i in range(OL):
+        h, rows = i // 3, pl.ds((i % 3) * OT, OT)
+        tt[h, rows, :] = (tt[h, rows, :] + selected(turned[h, rows, :], sel)) * inverse[h, rows, :]
+    def write(h, n):
+        place = pl.ds(pl.multiple_of(h * HIJ + n * OT, OT), OT)
+        return pltpu.make_async_copy(tt.at[h, bands[n]], out_ref.at[place], osem.at[h, n])
+
+    for n, rows in enumerate(bands):
+        tt[yh, rows, :] = oacc[yh, rows, :] * inverse[yh, rows, :] + tt[yh, rows, :]
+        write(yh, n).start()
+
+    for copy in x1 + x1b + x2 + ly + lz + lz2 + lc + direct + sum(first_hop + second_hop, []) + yr:
+        copy.wait_send()
+    for n, rows in enumerate(bands):
+        other_half = lad.at[1 - yh, rows]
+        rc(oacc.at[yh, rows], other_half, (OB, LY + 2, BACK)[n], opp).wait_recv()
+        tt[1 - yh, rows, :] = lad[1 - yh, rows, :] * inverse[1 - yh, rows, :] + tt[1 - yh, rows, :]
+        write(1 - yh, n).start()
+    for copy in ob:
+        copy.wait_send()
+    for n in range(OL // 2):
+        write(yh, n).wait()
+        write(1 - yh, n).wait()
 
 
 def to_peers():
@@ -475,11 +507,12 @@
         kernel,
         out_shape=jax.ShapeDtypeStruct((OL * OT, AB), F32),
         in_specs=[smem] * 3 + [anywhere, vmem, anywhere] + [vmem] * 6,
-        out_specs=vmem,
+        out_specs=anywhere,
         scratch_shapes=[
             pltpu.VMEM((1, AB), F32),
             pltpu.VMEM((OT, 1), F32),
             pltpu.VMEM((2, HIJ, AB), F32),
+            pltpu.VMEM((2, HIJ, AB // 2), F32),
             pltpu.VMEM((2, HIJ, AB), F32),
             pltpu.VMEM((AB, OL * OT), F32),
             pltpu.VMEM((4, 2, HIJ, AB), F32),
@@ -506,6 +539,7 @@
             pltpu.SemaphoreType.DMA((NSEM,)),
             pltpu.SemaphoreType.DMA((2,)),
             pltpu.SemaphoreType.DMA((6,)),
+            pltpu.SemaphoreType.DMA((2, 3)),
         ],
         compiler_params=pltpu.CompilerParams(
             collective_id=0, has_side_effects=True, vmem_limit_bytes=67043328

time: 147 us -> 145 us (0.986)
  no operation moved by 1% of the time
where the time goes in v5:
time: 145 us
  Pallas kernels  142 us (98%)
  local copies, waits for them, and re-layouts  2.36 us (2%)
    pallas_call x1, Pallas kernels, body(): pl.pallas_call(kernel, out_shape=jax.ShapeDtypeStruct((OL * OT, AB), F32)...  142 us

profile of v5, /device:TPU:0, one launch (start us, length us, event | category | flops | bytes accessed | tf_op | source)
XLA Modules:
  0.0 144.5 jit_solution(12507097146340406972)
XLA Ops:
  0.0 142.2 %shard_map.91 = f32[576,512]{1,0:T(8,128)} custom-call(s32[64]{0:T(128)} %virt_ref.1, f32[64]{0:T(128)} %ve_ref.1, f32[96]{0:T(128)} %oe_ref.1, f32[2,288,512]{2,1,0:T(8,128)} %bitcast.11, f32[512,256]{1,0:T(8,128)} %l_ref.1, f32[8,768,768]{2,1,0:T(8,128)} %bitcast.9, s32[1,64]{1,0:T(1,128)} %bitcast.12, s32[1,96]{1,0:T(1,128)} %bitcast.15, ...), custom_call_target="tpu_custom_call" | custom-call | tf_op jit(solution)/shard_map/pallas_call | solution.py:506
  142.2 2.4 %copy.11 = f32[512,576]{0,1:T(8,128)} copy(f32[512,576]{0,1:T(8,128)} %bitcast.10) | data formatting | bytes 2359296

commit v6 on v5

--- a/solution.py
+++ b/solution.py
@@ -297,10 +297,10 @@
     cyc(0)
     direct[0].start()
     pass_on(1 - yh, 1)
+    cyc(1)
+    direct[1].start()
     over_z(0)
     over_z(1)
-    cyc(1)
-    direct[1].start()
     cyc(2)
     direct[2].start()
 

time: 145 us -> 167 us (1.15)
  Pallas kernels: 142 us -> 165 us
    pallas_call x1, Pallas kernels: 142 us -> 165 us  [body(): pl.pallas_call(kernel, out_shape=jax.ShapeDtypeStruct((OL * OT, AB), F32)...]
where the time goes in v6:
time: 167 us
  Pallas kernels  165 us (99%)
  local copies, waits for them, and re-layouts  2.36 us (1%)
    pallas_call x1, Pallas kernels, body(): pl.pallas_call(kernel, out_shape=jax.ShapeDtypeStruct((OL * OT, AB), F32)...  165 us

profile of v6, /device:TPU:0, one launch (start us, length us, event | category | flops | bytes accessed | tf_op | source)
XLA Modules:
  0.0 167.2 jit_solution(16052827728926512234)
XLA Ops:
  0.0 164.8 %shard_map.91 = f32[576,512]{1,0:T(8,128)} custom-call(s32[64]{0:T(128)} %virt_ref.1, f32[64]{0:T(128)} %ve_ref.1, f32[96]{0:T(128)} %oe_ref.1, f32[2,288,512]{2,1,0:T(8,128)} %bitcast.11, f32[512,256]{1,0:T(8,128)} %l_ref.1, f32[8,768,768]{2,1,0:T(8,128)} %bitcast.9, s32[1,64]{1,0:T(1,128)} %bitcast.12, s32[1,96]{1,0:T(1,128)} %bitcast.15, ...), custom_call_target="tpu_custom_call" | custom-call | tf_op jit(solution)/shard_map/pallas_call | solution.py:506
  164.8 2.4 %copy.11 = f32[512,576]{0,1:T(8,128)} copy(f32[512,576]{0,1:T(8,128)} %bitcast.10) | data formatting | bytes 2359296
